TPU v7x, 256 devices: a whole 4x4x8 slice. The times are simulated.
256 devices in a mesh: dp: 8 (over y, core), expert: 32 (over z, x).
Axes of the slice: x: 4, y: 4, z: 8, core: 2. Of those that a mesh axis runs over, the one named last changes fastest.
Arguments:
- qkv: bfloat16 [256, 128, 6144], P(('dp', 'expert')), may hold values from -6 to 6
- resid: bfloat16 [256, 128, 2048], P(('dp', 'expert')), may hold values from -54 to 54
- lengths: int32 [256], P(('dp', 'expert')), may hold values from 32 to 128
- norm_gain: float32 [2048], replicated, may hold values from 0.25 to 1.75
- expert_ids: int32 [256, 128, 2], P(('dp', 'expert')), may hold values from 0 to 31, all different within a row; in each aligned block of 128 rows (0 to 127, 128 to 255, ..., all dimensions but the last counted through in order) at most 16 rows name the same one
- gate_vals: bfloat16 [256, 128, 2], P(('dp', 'expert')), may hold values from 0.099609375 to 1
- w_gate: bfloat16 [32, 768, 2048], P('expert', None, 'dp'), may hold values from -0.125 to 0.125
- w_up: bfloat16 [32, 768, 2048], P('expert', None, 'dp'), may hold values from -0.125 to 0.125
- w_down: bfloat16 [32, 768, 2048], P('expert', None, 'dp'), may hold values from -0.21875 to 0.21875
- cotangent: bfloat16 [256, 128, 2048], P(('dp', 'expert')), may hold values from -6 to 6
Outputs:
- mixture: bfloat16 [256, 128, 2048], P(('dp', 'expert'))
- grad_stream: float32 [256, 128, 2048], P(('dp', 'expert'))
- grad_gate: float32 [32, 768, 2048], P('expert', None, 'dp')
- grad_up: float32 [32, 768, 2048], P('expert', None, 'dp')
- grad_down: float32 [32, 768, 2048], P('expert', None, 'dp')
Inputs may be any that keep to these rules, and one draw needn't show every extreme that they name: `expert_ids`: among the 128 tokens of one device, no expert is named by more than 16 routes, a bound that some block reaches; the 2 ids of a token differ.
All inputs are finite; a program needn't handle non-finite values.
Results may differ from a plain program's by a relative error of at most 0.015.
Values may be sent and summed in bfloat16 or wider, within the bound.
No kernel may reach another device: no remote copies, remote signals or barrier semaphores. Data moves between devices by JAX's collectives and lax.ppermute only.
A program may use at most 128 MiB of HBM per device.

v0:
```python
import functools
import math

import jax
import jax.numpy as jnp
from jax import lax
from jax.experimental import pallas as pl
from jax.experimental.pallas import tpu as pltpu
from jax.sharding import PartitionSpec as P

HEADS = 16
ABSENT = 100.0
F32 = jnp.float32
BF16 = jnp.bfloat16
VMEM_LIMIT = 40 * 1024 * 1024


def cost(flops, bytes_accessed, transcendentals=0):
    return pl.CostEstimate(
        flops=flops, bytes_accessed=bytes_accessed, transcendentals=transcendentals
    )


def params():
    return pltpu.CompilerParams(vmem_limit_bytes=VMEM_LIMIT)


def dot_nt(a, b):
    return lax.dot_general(a, b, (((1,), (1,)), ((), ())), preferred_element_type=F32)


def dot_nn(a, b):
    return lax.dot_general(a, b, (((1,), (0,)), ((), ())), preferred_element_type=F32)


def pack_kernel(quarters, lengths_ref, qkv_ref, out_ref):
    rows = qkv_ref.shape[1]
    wide = out_ref.shape[3]
    step = pl.program_id(0)
    for block in range(rows // 16):
        times = step * rows + block * 16 + lax.broadcasted_iota(jnp.int32, (16, wide), 0)
        live = times < lengths_ref[0]
        for quarter in range(quarters):
            for kind in range(3):
                start = (kind * quarters + quarter) * wide
                piece = qkv_ref[0, block * 16 : block * 16 + 16, start : start + wide]
                if kind == 1:
                    piece = jnp.where(live, piece.astype(F32), ABSENT).astype(BF16)
                out_ref[block * quarters + quarter, kind] = piece


def pack(lengths, qkv, quarters):
    _, steps, triple = qkv.shape
    wide = triple // 3 // quarters
    rows = 32
    return pl.pallas_call(
        functools.partial(pack_kernel, quarters),
        grid=(steps // rows,),
        in_specs=[
            pl.BlockSpec(memory_space=pltpu.SMEM),
            pl.BlockSpec((1, rows, triple), lambda i: (0, i, 0)),
        ],
        out_specs=pl.BlockSpec((rows // 16 * quarters, 3, 16, wide), lambda i: (i, 0, 0, 0)),
        out_shape=jax.ShapeDtypeStruct((steps // 16 * quarters, 3, 16, wide), BF16),
        compiler_params=params(),
        cost_estimate=cost(0, 4 * steps * triple),
        name="pack_qkv",
    )(lengths, qkv)


def attend_kernel(head_size, scale, in_ref, out_ref):
    series, _, times, wide = in_ref.shape
    pairs = series * times
    chunk = 128
    for head in range(wide // head_size):
        lanes = slice(head * head_size, (head + 1) * head_size)
        keys = in_ref[:, 1, :, lanes].reshape(pairs, head_size)
        values = in_ref[:, 2, :, lanes].reshape(pairs, head_size)
        total = dot_nt(jnp.ones((8, head_size), BF16), keys)[0:1]
        live = total < 0.5 * ABSENT * head_size
        for part in range(pairs // chunk):
            first = part * chunk // times
            count = chunk // times
            queries = in_ref[first : first + count, 0, :, lanes].reshape(chunk, head_size)
            scores = dot_nt(queries, keys) * scale
            row = part * chunk + lax.broadcasted_iota(jnp.int32, (chunk, pairs), 0)
            column = lax.broadcasted_iota(jnp.int32, (chunk, pairs), 1)
            allowed = (((row ^ column) & (times - 1)) == 0) & (live | (row == column))
            scores = jnp.where(allowed, scores, -1e30)
            highest = jnp.max(scores, axis=1, keepdims=True)
            raised = jnp.exp(scores - highest)
            weights = (raised / jnp.sum(raised, axis=1, keepdims=True)).astype(BF16)
            attended = dot_nn(weights, values).astype(BF16)
            out_ref[first : first + count, :, lanes] = attended.reshape(count, times, head_size)


def attend(received, head_size):
    series, _, times, wide = received.shape
    pairs = series * times
    heads = wide // head_size
    return pl.pallas_call(
        functools.partial(attend_kernel, head_size, 1.0 / math.sqrt(head_size)),
        out_shape=jax.ShapeDtypeStruct((series, times, wide), BF16),
        compiler_params=params(),
        cost_estimate=cost(
            4 * heads * pairs * pairs * head_size, received.size * 8 // 3, heads * pairs * pairs
        ),
        name="attend",
    )(received)


def route_kernel(capacity, ids_ref, gates_ref, cotangent_ref, put_ref, take_ref, mix_ref, send_ref):
    tokens = ids_ref.shape[1]
    slots = put_ref.shape[0]
    ids = ids_ref[0]
    gates = gates_ref[0].astype(F32)
    lane = lax.broadcasted_iota(jnp.int32, (tokens, tokens), 1)
    sub = lax.broadcasted_iota(jnp.int32, (tokens, tokens), 0)
    named = [(lane == ids[:, k : k + 1]).astype(F32) for k in range(2)]
    earlier = (lane < sub).astype(BF16)
    before = dot_nn(earlier, (named[0] + named[1]).astype(BF16))
    slot = [
        ids[:, k : k + 1].astype(F32) * capacity
        + jnp.sum(before * named[k], axis=1, keepdims=True)
        for k in range(2)
    ]
    flat = [jnp.transpose(jnp.broadcast_to(slot[k], (tokens, tokens)))[0:1] for k in range(2)]
    flat_gate = [
        jnp.transpose(jnp.broadcast_to(gates[:, k : k + 1], (tokens, tokens)))[0:1]
        for k in range(2)
    ]
    along = lax.broadcasted_iota(jnp.int32, (tokens, slots), 1).astype(F32)
    down = lax.broadcasted_iota(jnp.int32, (slots, tokens), 0).astype(F32)
    hit = [along == slot[k] for k in range(2)]
    take_ref[...] = jnp.where(hit[0] | hit[1], 1.0, 0.0).astype(BF16)
    mix_ref[...] = jnp.where(
        hit[0], gates[:, 0:1], jnp.where(hit[1], gates[:, 1:2], 0.0)
    ).astype(BF16)
    fall = [down == flat[k] for k in range(2)]
    put_ref[...] = jnp.where(fall[0] | fall[1], 1.0, 0.0).astype(BF16)
    weigh = jnp.where(fall[0], flat_gate[0], jnp.where(fall[1], flat_gate[1], 0.0)).astype(BF16)
    wide = cotangent_ref.shape[2]
    for start in range(0, wide, 512):
        send_ref[:, start : start + 512] = dot_nn(
            weigh, cotangent_ref[0, :, start : start + 512]
        ).astype(BF16)


def route(ids, gates, cotangent, capacity, slots):
    _, tokens, wide = cotangent.shape
    return pl.pallas_call(
        functools.partial(route_kernel, capacity),
        out_shape=(
            jax.ShapeDtypeStruct((slots, tokens), BF16),
            jax.ShapeDtypeStruct((tokens, slots), BF16),
            jax.ShapeDtypeStruct((tokens, slots), BF16),
            jax.ShapeDtypeStruct((slots, wide), BF16),
        ),
        compiler_params=params(),
        cost_estimate=cost(2 * slots * tokens * wide, 2 * (slots + tokens) * wide),
        name="route",
    )(ids, gates, cotangent)


def norm_kernel(quarters, lengths_ref, att_ref, resid_ref, gain_ref, put_ref, stream_ref, inverse_ref, send_ref):
    blocks, times, wide = att_ref.shape
    for block in range(blocks):
        at, quarter = block // quarters, block % quarters
        rows = slice(at * times, (at + 1) * times)
        lanes = slice(quarter * wide, (quarter + 1) * wide)
        live = at * times + lax.broadcasted_iota(jnp.int32, (times, wide), 0) < lengths_ref[0]
        stream_ref[rows, lanes] = resid_ref[0, rows, lanes].astype(F32) + jnp.where(
            live, att_ref[block].astype(F32), 0.0
        )
    width = stream_ref.shape[1]
    stream = stream_ref[...]
    inverse = 1.0 / jnp.sqrt(jnp.sum(stream * stream, axis=1, keepdims=True) / width + 1e-05)
    inverse_ref[...] = jnp.broadcast_to(inverse, inverse_ref.shape)
    for start in range(0, width, 512):
        lanes = slice(start, start + 512)
        normed = (stream_ref[:, lanes] * inverse * gain_ref[:, lanes]).astype(BF16)
        send_ref[:, lanes] = dot_nn(put_ref[...], normed).astype(BF16)


def norm(lengths, att, resid, gain, put, quarters):
    _, tokens, width = resid.shape
    slots = put.shape[0]
    vmem = pl.BlockSpec(memory_space=pltpu.VMEM)
    return pl.pallas_call(
        functools.partial(norm_kernel, quarters),
        in_specs=[pl.BlockSpec(memory_space=pltpu.SMEM), vmem, vmem, vmem, vmem],
        out_shape=(
            jax.ShapeDtypeStruct((tokens, width), F32),
            jax.ShapeDtypeStruct((tokens, 128), F32),
            jax.ShapeDtypeStruct((slots, width), BF16),
        ),
        compiler_params=params(),
        cost_estimate=cost(2 * slots * tokens * width, 2 * (slots + 4 * tokens) * width),
        name="norm",
    )(lengths, att, resid, gain, put)


def expert_kernel(x_ref, gh_ref, gate_ref, up_ref, down_ref, out_ref, hidden_ref, gg_ref, gu_ref, acc_ref):
    step = pl.program_id(0)
    gate_pre = dot_nt(x_ref[...], gate_ref[0])
    up_pre = dot_nt(x_ref[...], up_ref[0])
    sigmoid = 1.0 / (1.0 + jnp.exp(-gate_pre))
    silu = gate_pre * sigmoid
    hidden = (silu * up_pre).astype(BF16)
    hidden_ref[...] = hidden
    product = dot_nn(hidden, down_ref[0])

    @pl.when(step == 0)
    def _():
        acc_ref[...] = product

    @pl.when((step > 0) & (step < pl.num_programs(0) - 1))
    def _():
        acc_ref[...] += product

    @pl.when(step == pl.num_programs(0) - 1)
    def _():
        out_ref[...] = (acc_ref[...] + product).astype(BF16)

    grad_hidden = gh_ref[...]
    gg_ref[...] = (grad_hidden * up_pre * sigmoid * (1.0 + gate_pre * (1.0 - sigmoid))).astype(BF16)
    gu_ref[...] = (grad_hidden * silu).astype(BF16)


def expert(x, grad_hidden, gate, up, down):
    rows, width = x.shape
    units = gate.shape[1]
    block = 256
    weight = pl.BlockSpec((1, block, width), lambda i: (0, i, 0))
    column = pl.BlockSpec((rows, block), lambda i: (0, i))
    whole = pl.BlockSpec((rows, width), lambda i: (0, 0))
    return pl.pallas_call(
        expert_kernel,
        grid=(units // block,),
        in_specs=[whole, column, weight, weight, weight],
        out_specs=(whole, column, column, column),
        out_shape=(
            jax.ShapeDtypeStruct((rows, width), BF16),
            jax.ShapeDtypeStruct((rows, units), BF16),
            jax.ShapeDtypeStruct((rows, units), BF16),
            jax.ShapeDtypeStruct((rows, units), BF16),
        ),
        scratch_shapes=[pltpu.VMEM((rows, width), F32)],
        compiler_params=pltpu.CompilerParams(
            dimension_semantics=("arbitrary",), vmem_limit_bytes=VMEM_LIMIT
        ),
        cost_estimate=cost(
            6 * rows * width * units, 4 * rows * width + 6 * units * width, rows * units
        ),
        name="expert",
    )(x, grad_hidden, gate, up, down)


def finish_kernel(take_ref, home_ref, stream_ref, inverse_ref, gain_ref, out_ref):
    width = stream_ref.shape[1]
    inverse = inverse_ref[:, 0:1]
    total = 0.0
    for start in range(0, width, 512):
        lanes = slice(start, start + 512)
        scaled = dot_nn(take_ref[...], home_ref[:, lanes]) * gain_ref[:, lanes]
        out_ref[0, :, lanes] = scaled
        total = total + jnp.sum(stream_ref[:, lanes] * scaled, axis=1, keepdims=True)
    factor = inverse * inverse * inverse * (total / width)
    out_ref[0] = inverse * out_ref[0] - stream_ref[...] * factor


def finish(take, home, stream, inverse, gain):
    tokens, width = stream.shape
    slots = home.shape[0]
    return pl.pallas_call(
        finish_kernel,
        out_shape=jax.ShapeDtypeStruct((1, tokens, width), F32),
        compiler_params=params(),
        cost_estimate=cost(2 * slots * tokens * width, 2 * (slots + 4 * tokens) * width),
        name="finish",
    )(take, home, stream, inverse, gain)


def swap(values, axis="expert"):
    return lax.all_to_all(values, axis, split_axis=0, concat_axis=0, tiled=True)


def body(qkv, resid, lengths, norm_gain, expert_ids, gate_vals, w_gate, w_up, w_down, cotangent):
    _, steps, triple = qkv.shape
    width = triple // 3
    head_size = width // HEADS
    owners = lax.axis_size("expert")
    quarters = owners // (steps // 16)
    capacity = 2 * steps * expert_ids.shape[2] // owners
    slots = owners * capacity
    gain = norm_gain.reshape(1, width)

    down_full = lax.all_gather(w_down, "dp", axis=2, tiled=True)
    gate_full = lax.all_gather(w_gate, "dp", axis=2, tiled=True)
    up_full = lax.all_gather(w_up, "dp", axis=2, tiled=True)

    received = swap(pack(lengths, qkv, quarters))
    put, take, mix, adjoint_send = route(expert_ids, gate_vals, cotangent, capacity, slots)
    grad_out = swap(adjoint_send.reshape(owners, capacity, width)).reshape(slots, width)
    att_home = swap(attend(received, head_size))
    stream, inverse, normed_send = norm(lengths, att_home, resid, gain, put, quarters)
    x_rows = swap(normed_send.reshape(owners, capacity, width)).reshape(slots, width)

    grad_hidden = dot_nt(grad_out, down_full[0])
    expert_out, hidden, grad_gate_pre, grad_up_pre = expert(
        x_rows, grad_hidden, gate_full, up_full, down_full
    )
    out_home = swap(expert_out.reshape(owners, capacity, width)).reshape(slots, width)

    def weight_grad(left, right):
        part = lax.dot_general(left, right, (((0,), (0,)), ((), ())), preferred_element_type=F32)
        return lax.psum_scatter(
            part.astype(BF16)[None], "dp", scatter_dimension=2, tiled=True
        ).astype(F32)

    grad_gate = weight_grad(grad_gate_pre, x_rows)
    grad_up = weight_grad(grad_up_pre, x_rows)
    grad_down = weight_grad(hidden, grad_out)
    grad_rows = (dot_nn(grad_gate_pre, gate_full[0]) + dot_nn(grad_up_pre, up_full[0])).astype(BF16)
    grad_home = swap(grad_rows.reshape(owners, capacity, width)).reshape(slots, width)

    mixture = dot_nn(mix, out_home).astype(BF16)[None]
    grad_stream = finish(take, grad_home, stream, inverse, gain)
    return (mixture, grad_stream, grad_gate, grad_up, grad_down)


def solution(mesh):
    tokens = P(("dp", "expert"), None, None)
    weights = P("expert", None, "dp")
    in_specs = (
        tokens,
        tokens,
        P(("dp", "expert")),
        P(),
        tokens,
        tokens,
        weights,
        weights,
        weights,
        tokens,
    )
    out_specs = (tokens, tokens, weights, weights, weights)
    return jax.shard_map(body, mesh=mesh, in_specs=in_specs, out_specs=out_specs, check_vma=False)
```

profile of v0, /device:TPU:16, one launch (start us, length us, event | category | flops | bytes accessed | tf_op | source)
XLA Modules:
  0.0 356.5 jit_solution(9993181244641848377)
XLA Ops:
  8.6 1.4 copy-done.3
  10.0 1.8 pack_qkv.1
  11.7 11.3 %all-to-all-start = ((bf16[32,3,16,512]{3,2,1,0:T(8,128)(2,1)}), bf16[32,3,16,512]{3,2,1,0:T(8,128)(2,1)S(1)}, u32[]{:S(2)}, u32[]{:S(2)}) async-start(bf16[32,3,16,512]{3,2,1,0:T(8,128)(2,1)} %pack_qkv.1), calls=%async_computation | async-start | bytes 3145728 | tf_op jit(solution)/shard_map/all_to_all | solution.py:285
  23.8 38.3 %all-to-all-done.in_ref = bf16[32,3,16,512]{3,2,1,0:T(8,128)(2,1)S(1)} async-done(((bf16[32,3,16,512]{3,2,1,0:T(8,128)(2,1)}), bf16[32,3,16,512]{3,2,1,0:T(8,128)(2,1)S(1)}, u32[]{:S(2)}, u32[]{:S(2)}) %all-to-all-start) | async-done | bytes 1572896 | tf_op jit(solution)/shard_map/all_to_all | solution.py:285
  62.1 6.8 %attend.1 = bf16[32,16,512]{2,1,0:T(8,128)(2,1)} custom-call(bf16[32,3,16,512]{3,2,1,0:T(8,128)(2,1)S(1)} %all-to-all-done.in_ref), custom_call_target="tpu_custom_call" | custom-call | flops 536870912 | bytes 2097152 | tf_op jit(solution)/shard_map/attend/pallas_call | solution.py:101
  69.0 5.8 %all-to-all-start.1 = ((bf16[32,16,512]{2,1,0:T(8,128)(2,1)}), bf16[32,16,512]{2,1,0:T(8,128)(2,1)S(1)}, u32[]{:S(2)}, u32[]{:S(2)}) async-start(bf16[32,16,512]{2,1,0:T(8,128)(2,1)} %attend.1), calls=%async_computation.1 | async-start | bytes 1048576 | tf_op jit(solution)/shard_map/all_to_all | solution.py:285
  75.0 2.6 route.1
  77.6 13.8 %all-to-all-done.1.att_ref = bf16[32,16,512]{2,1,0:T(8,128)(2,1)S(1)} async-done(((bf16[32,16,512]{2,1,0:T(8,128)(2,1)}), bf16[32,16,512]{2,1,0:T(8,128)(2,1)S(1)}, u32[]{:S(2)}, u32[]{:S(2)}) %all-to-all-start.1) | async-done | bytes 524320 | tf_op jit(solution)/shard_map/all_to_all | solution.py:285
  91.4 4.9 %all-to-all-start.3 = ((bf16[32,16,2048]{2,1,0:T(8,128)(2,1)}), bf16[32,16,2048]{2,1,0:T(8,128)(2,1)}, u32[]{:S(2)}, u32[]{:S(2)}) async-start(bf16[32,16,2048]{2,1,0:T(8,128)(2,1)} %bitcast.3), calls=%async_computation.3 | async-start | bytes 4194304 | tf_op jit(solution)/shard_map/all_to_all | solution.py:285
  98.1 1.3 copy-done.2
  99.4 45.5 %all-to-all-done.3 = bf16[32,16,2048]{2,1,0:T(8,128)(2,1)} async-done(((bf16[32,16,2048]{2,1,0:T(8,128)(2,1)}), bf16[32,16,2048]{2,1,0:T(8,128)(2,1)}, u32[]{:S(2)}, u32[]{:S(2)}) %all-to-all-start.3) | async-done | bytes 2097184 | tf_op jit(solution)/shard_map/all_to_all | solution.py:285
  144.9 5.9 %all-to-all-start.2 = ((bf16[32,16,2048]{2,1,0:T(8,128)(2,1)}), bf16[32,16,2048]{2,1,0:T(8,128)(2,1)S(1)}, u32[]{:S(2)}, u32[]{:S(2)}) async-start(bf16[32,16,2048]{2,1,0:T(8,128)(2,1)} %bitcast.44), calls=%async_computation.2 | async-start | bytes 4194304 | tf_op jit(solution)/shard_map/all_to_all | solution.py:285
  151.1 5.6 %fusion.4.gh_ref = f32[512,768]{1,0:T(8,128)} fusion(bf16[512,2048]{1,0:T(8,128)(2,1)} %bitcast.4, bf16[1,768,2048]{2,1,0:T(8,128)(2,1)} %all-gather.4.cloned.1.call-done.down_ref), kind=kOutput, calls=%fused_computation.8 | convolution fusion | flops 1610612736 | bytes 6815744 | tf_op jit(solution)/shard_map/dot_general | solution.py:29
  156.7 41.8 %all-to-all-done.2 = bf16[32,16,2048]{2,1,0:T(8,128)(2,1)S(1)} async-done(((bf16[32,16,2048]{2,1,0:T(8,128)(2,1)}), bf16[32,16,2048]{2,1,0:T(8,128)(2,1)S(1)}, u32[]{:S(2)}, u32[]{:S(2)}) %all-to-all-start.2) | async-done | bytes 2097184 | tf_op jit(solution)/shard_map/all_to_all | solution.py:285
  198.5 2.6 copy-done.6
  201.1 1.9 copy-done.8
  203.0 1.4 copy-done.14
  204.4 8.6 %expert.1 = (bf16[512,2048]{1,0:T(8,128)(2,1)S(1)}, bf16[512,768]{1,0:T(8,128)(2,1)S(1)}, bf16[512,768]{1,0:T(8,128)(2,1)S(1)}, bf16[512,768]{1,0:T(8,128)(2,1)S(1)}) custom-call(bf16[512,2048]{1,0:T(8,128)(2,1)S(1)} %bitcast.41, f32[512,768]{1,0:T(8,128)S(1)} %copy-done.14, bf16[1,768,2048]{2,1,0:T(8,128)(2,1)S(1)} %copy-done.6, ...), custom_call_target="tpu_custom_call" | custom-call | flops 4831838208 | bytes 13631488 | tf_op jit(solution)/shard_map/expert/pallas_call | solution.py:237
  216.1 5.1 %fusion.8 = bf16[1,768,2048]{2,1,0:T(8,128)(2,1)} fusion(bf16[512,768]{1,0:T(8,128)(2,1)S(1)} %get-tuple-element.26, bf16[512,2048]{1,0:T(8,128)(2,1)} %bitcast.4), kind=kOutput, calls=%fused_computation.12 | convolution fusion | flops 1612185600 | bytes 6029312 | tf_op jit(solution)/shard_map/dot_general | solution.py:316
  221.3 4.7 %fusion.7 = bf16[1,768,2048]{2,1,0:T(8,128)(2,1)} fusion(bf16[512,768]{1,0:T(8,128)(2,1)} %copy-done.12, bf16[512,2048]{1,0:T(8,128)(2,1)S(1)} %bitcast.42), kind=kOutput, calls=%fused_computation.11 | convolution fusion | flops 1612185600 | bytes 6029312 | tf_op jit(solution)/shard_map/dot_general | solution.py:316
  227.1 3.9 %fusion = f32[512,2048]{1,0:T(8,128)S(1)} fusion(bf16[512,768]{1,0:T(8,128)(2,1)S(1)} %copy-done.13, bf16[1,768,2048]{2,1,0:T(8,128)(2,1)} %all-gather.8.cloned.1.call-done.up_ref), kind=kOutput, calls=%fused_computation.4 | convolution fusion | flops 1610612736 | bytes 8126464 | tf_op jit(solution)/shard_map/dot_general | solution.py:33
  231.0 3.2 add_convert_fusion
  234.2 5.9 %all-to-all-start.5 = ((bf16[32,16,2048]{2,1,0:T(8,128)(2,1)}), bf16[32,16,2048]{2,1,0:T(8,128)(2,1)S(1)}, u32[]{:S(2)}, u32[]{:S(2)}) async-start(bf16[32,16,2048]{2,1,0:T(8,128)(2,1)} %bitcast.47), calls=%async_computation.5 | async-start | bytes 4194304 | tf_op jit(solution)/shard_map/all_to_all | solution.py:285
  240.4 5.3 %fusion.6 = bf16[1,768,2048]{2,1,0:T(8,128)(2,1)} fusion(bf16[512,768]{1,0:T(8,128)(2,1)} %copy-done.10, bf16[512,2048]{1,0:T(8,128)(2,1)} %bitcast.43), kind=kOutput, calls=%fused_computation.10 | convolution fusion | flops 1612185600 | bytes 6029312 | tf_op jit(solution)/shard_map/dot_general | solution.py:316
  245.8 41.8 %all-to-all-done.5 = bf16[32,16,2048]{2,1,0:T(8,128)(2,1)S(1)} async-done(((bf16[32,16,2048]{2,1,0:T(8,128)(2,1)}), bf16[32,16,2048]{2,1,0:T(8,128)(2,1)S(1)}, u32[]{:S(2)}, u32[]{:S(2)}) %all-to-all-start.5) | async-done | bytes 2097184 | tf_op jit(solution)/shard_map/all_to_all | solution.py:285
  287.6 6.1 %all-to-all-start.4 = ((bf16[32,16,2048]{2,1,0:T(8,128)(2,1)}), bf16[32,16,2048]{2,1,0:T(8,128)(2,1)}, u32[]{:S(2)}, u32[]{:S(2)}) async-start(bf16[32,16,2048]{2,1,0:T(8,128)(2,1)} %bitcast.40), calls=%async_computation.4 | async-start | bytes 4194304 | tf_op jit(solution)/shard_map/all_to_all | solution.py:285
  293.6 1.7 finish.1
  295.4 45.7 %all-to-all-done.4 = bf16[32,16,2048]{2,1,0:T(8,128)(2,1)} async-done(((bf16[32,16,2048]{2,1,0:T(8,128)(2,1)}), bf16[32,16,2048]{2,1,0:T(8,128)(2,1)}, u32[]{:S(2)}, u32[]{:S(2)}) %all-to-all-start.4) | async-done | bytes 2097184 | tf_op jit(solution)/shard_map/all_to_all | solution.py:285
  341.0 2.8 fusion.11
  343.9 1.9 convert_element_type.31
  345.8 1.9 convert_element_type.29
  347.7 1.9 convert_element_type.27
  (50 shorter events, 8.2 us)
Async XLA Ops:
  7.2 143.9 %all-gather.4.cloned.1.call-start = ((), (), s32[]{:S(2)}) async-start(), calls=%async_computation.9 | async-start | bytes 3538944 | tf_op jit(solution)/shard_map/all_gather | solution.py:298
  8.5 1.4 copy-start.3
  11.7 50.4 %all-to-all-start = ((bf16[32,3,16,512]{3,2,1,0:T(8,128)(2,1)}), bf16[32,3,16,512]{3,2,1,0:T(8,128)(2,1)S(1)}, u32[]{:S(2)}, u32[]{:S(2)}) async-start(bf16[32,3,16,512]{3,2,1,0:T(8,128)(2,1)} %pack_qkv.1), calls=%async_computation | async-start | bytes 3145728 | tf_op jit(solution)/shard_map/all_to_all | solution.py:285
  23.0 51.7 %copy-start.16 = (bf16[1,128,2]{1,2,0:T(2,128)(2,1)S(1)}, bf16[1,128,2]{1,2,0:T(2,128)(2,1)}, u32[]{:S(2)}) copy-start(bf16[1,128,2]{1,2,0:T(2,128)(2,1)} %param.15) | copy-start | bytes 1540
  23.1 51.9 %copy-start.15 = (s32[1,128,2]{1,2,0:T(2,128)S(1)}, s32[1,128,2]{1,2,0:T(2,128)}, u32[]{:S(2)}) copy-start(s32[1,128,2]{1,2,0:T(2,128)} %param.14) | copy-start | bytes 3076
  23.1 52.0 %copy-start.9 = (bf16[1,128,2048]{2,1,0:T(8,128)(2,1)S(1)}, bf16[1,128,2048]{2,1,0:T(8,128)(2,1)}, u32[]{:S(2)}) copy-start(bf16[1,128,2048]{2,1,0:T(8,128)(2,1)} %cotangent_ref.1) | copy-start | bytes 1572868
  23.1 133.6 %all-gather.6.cloned.1.call-start = ((), (), s32[]{:S(2)}) async-start(), calls=%async_computation.10 | async-start | bytes 3538944 | tf_op jit(solution)/shard_map/all_gather | solution.py:299
  69.0 22.4 %all-to-all-start.1 = ((bf16[32,16,512]{2,1,0:T(8,128)(2,1)}), bf16[32,16,512]{2,1,0:T(8,128)(2,1)S(1)}, u32[]{:S(2)}, u32[]{:S(2)}) async-start(bf16[32,16,512]{2,1,0:T(8,128)(2,1)} %attend.1), calls=%async_computation.1 | async-start | bytes 1048576 | tf_op jit(solution)/shard_map/all_to_all | solution.py:285
  91.4 5.6 %copy-start.4 = (bf16[1,128,2048]{2,1,0:T(8,128)(2,1)S(1)}, bf16[1,128,2048]{2,1,0:T(8,128)(2,1)}, u32[]{:S(2)}) copy-start(bf16[1,128,2048]{2,1,0:T(8,128)(2,1)} %resid_ref.1) | copy-start | bytes 1572868
  91.4 5.7 %copy-start.5 = (f32[2048]{0:T(1024)S(1)}, f32[2048]{0:T(1024)}, u32[]{:S(2)}) copy-start(f32[2048]{0:T(1024)} %param.13) | copy-start | bytes 24580
  91.4 53.5 %all-to-all-start.3 = ((bf16[32,16,2048]{2,1,0:T(8,128)(2,1)}), bf16[32,16,2048]{2,1,0:T(8,128)(2,1)}, u32[]{:S(2)}, u32[]{:S(2)}) async-start(bf16[32,16,2048]{2,1,0:T(8,128)(2,1)} %bitcast.3), calls=%async_computation.3 | async-start | bytes 4194304 | tf_op jit(solution)/shard_map/all_to_all | solution.py:285
  96.3 60.4 %all-gather.8.cloned.1.call-start = ((), (), s32[]{:S(2)}) async-start(), calls=%async_computation.11 | async-start | bytes 3538944 | tf_op jit(solution)/shard_map/all_gather | solution.py:300
  98.1 1.3 copy-start.2
  144.9 53.6 %all-to-all-start.2 = ((bf16[32,16,2048]{2,1,0:T(8,128)(2,1)}), bf16[32,16,2048]{2,1,0:T(8,128)(2,1)S(1)}, u32[]{:S(2)}, u32[]{:S(2)}) async-start(bf16[32,16,2048]{2,1,0:T(8,128)(2,1)} %bitcast.44), calls=%async_computation.2 | async-start | bytes 4194304 | tf_op jit(solution)/shard_map/all_to_all | solution.py:285
  150.8 193.0 %reduce-scatter.8.cloned.1.call-start = ((), (), s32[]{:S(2)}) async-start(), calls=%async_computation.14 | async-start | bytes 3538944 | tf_op jit(solution)/shard_map/reduce_scatter | solution.py:317
  198.5 22.8 %copy-start.1 = (bf16[32,16,2048]{2,1,0:T(8,128)(2,1)}, bf16[32,16,2048]{2,1,0:T(8,128)(2,1)S(1)}, u32[]{:S(2)}) copy-start(bf16[32,16,2048]{2,1,0:T(8,128)(2,1)S(1)} %all-to-all-done.2) | copy-start | bytes 6291460
  198.5 2.6 copy-start.6
  201.1 1.9 copy-start.8
  203.0 1.4 copy-start.14
  213.0 1.3 copy-start
  214.3 0.9 copy-start.10
  215.2 0.9 copy-start.12
  221.2 124.6 %reduce-scatter.6.cloned.1.call-start = ((), (), s32[]{:S(2)}) async-start(), calls=%async_computation.13 | async-start | bytes 3538944 | tf_op jit(solution)/shard_map/reduce_scatter | solution.py:317
  226.0 1.1 copy-start.13
  227.1 3.9 %copy-start.7 = (bf16[1,768,2048]{2,1,0:T(8,128)(2,1)S(1)}, bf16[1,768,2048]{2,1,0:T(8,128)(2,1)}, u32[]{:S(2)}) copy-start(bf16[1,768,2048]{2,1,0:T(8,128)(2,1)} %all-gather.6.cloned.1.call-done.gate_ref) | copy-start | bytes 9437188
  227.1 3.9 %copy-start.11 = (bf16[512,768]{1,0:T(8,128)(2,1)S(1)}, bf16[512,768]{1,0:T(8,128)(2,1)}, u32[]{:S(2)}) copy-start(bf16[512,768]{1,0:T(8,128)(2,1)} %copy-done.10) | copy-start | bytes 2359300
  234.2 53.4 %all-to-all-start.5 = ((bf16[32,16,2048]{2,1,0:T(8,128)(2,1)}), bf16[32,16,2048]{2,1,0:T(8,128)(2,1)S(1)}, u32[]{:S(2)}, u32[]{:S(2)}) async-start(bf16[32,16,2048]{2,1,0:T(8,128)(2,1)} %bitcast.47), calls=%async_computation.5 | async-start | bytes 4194304 | tf_op jit(solution)/shard_map/all_to_all | solution.py:285
  240.2 107.6 %reduce-scatter.4.cloned.1.call-start = ((), (), s32[]{:S(2)}) async-start(), calls=%async_computation.12 | async-start | bytes 3538944 | tf_op jit(solution)/shard_map/reduce_scatter | solution.py:317
  287.6 53.5 %all-to-all-start.4 = ((bf16[32,16,2048]{2,1,0:T(8,128)(2,1)}), bf16[32,16,2048]{2,1,0:T(8,128)(2,1)}, u32[]{:S(2)}, u32[]{:S(2)}) async-start(bf16[32,16,2048]{2,1,0:T(8,128)(2,1)} %bitcast.40), calls=%async_computation.4 | async-start | bytes 4194304 | tf_op jit(solution)/shard_map/all_to_all | solution.py:285
Sparse Core Ops, SparseCore 0:
  9.8 36.6 all-gather.3
  48.4 35.2 all-gather.5
  99.0 35.0 all-gather.7
  221.3 30.8 reduce-scatter.7
  254.6 37.5 reduce-scatter.5
  294.6 37.4 reduce-scatter.3
where the time goes:
time: 358 us; the launch traced here: 357 us
  waiting for transfers between devices  229 us (64%)
  starting transfers between devices  40.6 us (11%)
  matrix products  30.6 us (9%)
  Pallas kernels  22.4 us (6%)
  between operations  14.9 us (4%)
  local copies, waits for them, and re-layouts  13.1 us (4%)
  other arithmetic  5.79 us (2%)
    all_to_all x6, waiting for transfers between devices, swap(): return lax.all_to_all(values, axis, split_axis=0, concat_axis=0, tiled=True)  227 us
    all_to_all x6, starting transfers between devices, swap(): return lax.all_to_all(values, axis, split_axis=0, concat_axis=0, tiled=True)  39.9 us
    dot_general x3, matrix products, weight_grad(): lax.dot_general(left, right, (((0,), (0,)), ((), ())), preferred_element_...  15.1 us
    unnamed x36, local copies, waits for them, and re-layouts  13.1 us
    dot_general x3, matrix products, dot_nn(): lax.dot_general(a, b, (((1,), (0,)), ((), ())), preferred_element_type=F32)  9.92 us
    pallas_call x1, Pallas kernels, expert(): pl.pallas_call(expert_kernel, grid=(units // block,), in_specs=[whole, co...  8.58 us
  transfers between devices with their start and end apart: 12, of which 6 were waited for; matrix products, arithmetic and copies ran while one was open for 8% of the time, Pallas kernels for 4%

commit v1 on v0

--- a/solution.py
+++ b/solution.py
@@ -27,6 +27,10 @@
 
 def dot_nt(a, b):
     return lax.dot_general(a, b, (((1,), (1,)), ((), ())), preferred_element_type=F32)
+
+
+def flat_rows(ref):
+    return ref[...].reshape(ref.shape[0] * ref.shape[1], ref.shape[2])
 
 
 def dot_nn(a, b):
@@ -68,7 +72,8 @@
     )(lengths, qkv)
 
 
-def attend_kernel(head_size, scale, in_ref, out_ref):
+def attend_kernel(head_size, scale, in_ref, shared_ref, out_ref):
+    del shared_ref
     series, _, times, wide = in_ref.shape
     pairs = series * times
     chunk = 128
@@ -94,19 +99,27 @@
             out_ref[first : first + count, :, lanes] = attended.reshape(count, times, head_size)
 
 
-def attend(received, head_size):
+def attend(received, shared, head_size):
     series, _, times, wide = received.shape
     pairs = series * times
     heads = wide // head_size
+    last = shared.shape[2] // wide - 1
     return pl.pallas_call(
         functools.partial(attend_kernel, head_size, 1.0 / math.sqrt(head_size)),
-        out_shape=jax.ShapeDtypeStruct((series, times, wide), BF16),
+        grid=(1,),
+        in_specs=[
+            pl.BlockSpec(received.shape, lambda i: (0, 0, 0, 0)),
+            pl.BlockSpec(memory_space=pl.ANY),
+        ],
+        out_specs=pl.BlockSpec((series, times, wide), lambda i: (0, 0, last)),
+        out_shape=jax.ShapeDtypeStruct(shared.shape, BF16),
+        input_output_aliases={1: 0},
         compiler_params=params(),
         cost_estimate=cost(
             4 * heads * pairs * pairs * head_size, received.size * 8 // 3, heads * pairs * pairs
         ),
         name="attend",
-    )(received)
+    )(received, shared)
 
 
 def route_kernel(capacity, ids_ref, gates_ref, cotangent_ref, put_ref, take_ref, mix_ref, send_ref):
@@ -139,14 +152,14 @@
     fall = [down == flat[k] for k in range(2)]
     put_ref[...] = jnp.where(fall[0] | fall[1], 1.0, 0.0).astype(BF16)
     weigh = jnp.where(fall[0], flat_gate[0], jnp.where(fall[1], flat_gate[1], 0.0)).astype(BF16)
+    owners = slots // capacity
     wide = cotangent_ref.shape[2]
     for start in range(0, wide, 512):
-        send_ref[:, start : start + 512] = dot_nn(
-            weigh, cotangent_ref[0, :, start : start + 512]
-        ).astype(BF16)
-
-
-def route(ids, gates, cotangent, capacity, slots):
+        rows = dot_nn(weigh, cotangent_ref[0, :, start : start + 512]).astype(BF16)
+        send_ref[:, :, start : start + 512] = rows.reshape(owners, capacity, 512)
+
+
+def route(ids, gates, cotangent, capacity, slots, extra):
     _, tokens, wide = cotangent.shape
     return pl.pallas_call(
         functools.partial(route_kernel, capacity),
@@ -154,7 +167,19 @@
             jax.ShapeDtypeStruct((slots, tokens), BF16),
             jax.ShapeDtypeStruct((tokens, slots), BF16),
             jax.ShapeDtypeStruct((tokens, slots), BF16),
-            jax.ShapeDtypeStruct((slots, wide), BF16),
+            jax.ShapeDtypeStruct((slots // capacity, capacity, wide + extra), BF16),
+        ),
+        grid=(1,),
+        in_specs=[
+            pl.BlockSpec(ids.shape, lambda i: (0, 0, 0)),
+            pl.BlockSpec(gates.shape, lambda i: (0, 0, 0)),
+            pl.BlockSpec(cotangent.shape, lambda i: (0, 0, 0)),
+        ],
+        out_specs=(
+            pl.BlockSpec((slots, tokens), lambda i: (0, 0)),
+            pl.BlockSpec((tokens, slots), lambda i: (0, 0)),
+            pl.BlockSpec((tokens, slots), lambda i: (0, 0)),
+            pl.BlockSpec((slots // capacity, capacity, wide), lambda i: (0, 0, 0)),
         ),
         compiler_params=params(),
         cost_estimate=cost(2 * slots * tokens * wide, 2 * (slots + tokens) * wide),
@@ -179,20 +204,34 @@
     for start in range(0, width, 512):
         lanes = slice(start, start + 512)
         normed = (stream_ref[:, lanes] * inverse * gain_ref[:, lanes]).astype(BF16)
-        send_ref[:, lanes] = dot_nn(put_ref[...], normed).astype(BF16)
+        rows = dot_nn(put_ref[...], normed).astype(BF16)
+        send_ref[:, :, lanes] = rows.reshape(send_ref.shape[0], send_ref.shape[1], 512)
 
 
 def norm(lengths, att, resid, gain, put, quarters):
     _, tokens, width = resid.shape
     slots = put.shape[0]
-    vmem = pl.BlockSpec(memory_space=pltpu.VMEM)
+    blocks, times, whole = att.shape
+    wide = width // quarters
     return pl.pallas_call(
         functools.partial(norm_kernel, quarters),
-        in_specs=[pl.BlockSpec(memory_space=pltpu.SMEM), vmem, vmem, vmem, vmem],
+        grid=(1,),
+        in_specs=[
+            pl.BlockSpec(memory_space=pltpu.SMEM),
+            pl.BlockSpec((blocks, times, wide), lambda i: (0, 0, whole // wide - 1)),
+            pl.BlockSpec(resid.shape, lambda i: (0, 0, 0)),
+            pl.BlockSpec(gain.shape, lambda i: (0, 0)),
+            pl.BlockSpec(put.shape, lambda i: (0, 0)),
+        ],
+        out_specs=(
+            pl.BlockSpec((tokens, width), lambda i: (0, 0)),
+            pl.BlockSpec((tokens, 128), lambda i: (0, 0)),
+            pl.BlockSpec((blocks, slots // blocks, width), lambda i: (0, 0, 0)),
+        ),
         out_shape=(
             jax.ShapeDtypeStruct((tokens, width), F32),
             jax.ShapeDtypeStruct((tokens, 128), F32),
-            jax.ShapeDtypeStruct((slots, width), BF16),
+            jax.ShapeDtypeStruct((blocks, slots // blocks, width), BF16),
         ),
         compiler_params=params(),
         cost_estimate=cost(2 * slots * tokens * width, 2 * (slots + 4 * tokens) * width),
@@ -200,14 +239,15 @@
     )(lengths, att, resid, gain, put)
 
 
-def expert_kernel(x_ref, gh_ref, gate_ref, up_ref, down_ref, out_ref, hidden_ref, gg_ref, gu_ref, acc_ref):
+def expert_kernel(x_ref, gh_ref, gate_ref, up_ref, down_ref, out_ref, inner_ref, acc_ref):
     step = pl.program_id(0)
-    gate_pre = dot_nt(x_ref[...], gate_ref[0])
-    up_pre = dot_nt(x_ref[...], up_ref[0])
+    x = flat_rows(x_ref)
+    gate_pre = dot_nt(x, gate_ref[0])
+    up_pre = dot_nt(x, up_ref[0])
     sigmoid = 1.0 / (1.0 + jnp.exp(-gate_pre))
     silu = gate_pre * sigmoid
     hidden = (silu * up_pre).astype(BF16)
-    hidden_ref[...] = hidden
+    inner_ref[2] = hidden
     product = dot_nn(hidden, down_ref[0])
 
     @pl.when(step == 0)
@@ -220,30 +260,31 @@
 
     @pl.when(step == pl.num_programs(0) - 1)
     def _():
-        out_ref[...] = (acc_ref[...] + product).astype(BF16)
+        out_ref[...] = (acc_ref[...] + product).astype(BF16).reshape(out_ref.shape)
 
     grad_hidden = gh_ref[...]
-    gg_ref[...] = (grad_hidden * up_pre * sigmoid * (1.0 + gate_pre * (1.0 - sigmoid))).astype(BF16)
-    gu_ref[...] = (grad_hidden * silu).astype(BF16)
+    inner_ref[0] = (
+        grad_hidden * up_pre * sigmoid * (1.0 + gate_pre * (1.0 - sigmoid))
+    ).astype(BF16)
+    inner_ref[1] = (grad_hidden * silu).astype(BF16)
 
 
 def expert(x, grad_hidden, gate, up, down):
-    rows, width = x.shape
+    owners, capacity, width = x.shape
+    rows = owners * capacity
     units = gate.shape[1]
     block = 256
     weight = pl.BlockSpec((1, block, width), lambda i: (0, i, 0))
     column = pl.BlockSpec((rows, block), lambda i: (0, i))
-    whole = pl.BlockSpec((rows, width), lambda i: (0, 0))
+    whole = pl.BlockSpec((owners, capacity, width), lambda i: (0, 0, 0))
     return pl.pallas_call(
         expert_kernel,
         grid=(units // block,),
         in_specs=[whole, column, weight, weight, weight],
-        out_specs=(whole, column, column, column),
+        out_specs=(whole, pl.BlockSpec((3, rows, block), lambda i: (0, 0, i))),
         out_shape=(
-            jax.ShapeDtypeStruct((rows, width), BF16),
-            jax.ShapeDtypeStruct((rows, units), BF16),
-            jax.ShapeDtypeStruct((rows, units), BF16),
-            jax.ShapeDtypeStruct((rows, units), BF16),
+            jax.ShapeDtypeStruct(x.shape, BF16),
+            jax.ShapeDtypeStruct((3, rows, units), BF16),
         ),
         scratch_shapes=[pltpu.VMEM((rows, width), F32)],
         compiler_params=pltpu.CompilerParams(
@@ -254,6 +295,137 @@
         ),
         name="expert",
     )(x, grad_hidden, gate, up, down)
+
+
+def grad_hidden_kernel(grad_out_ref, down_ref, out_ref):
+    out_ref[...] = dot_nt(flat_rows(grad_out_ref), down_ref[0])
+
+
+def hidden_grad(shared, down):
+    owners, capacity, _ = shared.shape
+    rows = owners * capacity
+    _, units, width = down.shape
+    block = 256
+    return pl.pallas_call(
+        grad_hidden_kernel,
+        grid=(units // block,),
+        in_specs=[
+            pl.BlockSpec((owners, capacity, width), lambda i: (0, 0, 0)),
+            pl.BlockSpec((1, block, width), lambda i: (0, i, 0)),
+        ],
+        out_specs=pl.BlockSpec((rows, block), lambda i: (0, i)),
+        out_shape=jax.ShapeDtypeStruct((rows, units), F32),
+        compiler_params=params(),
+        cost_estimate=cost(2 * rows * units * width, 2 * width * (rows + units) + 4 * rows * units),
+        name="grad_hidden",
+    )(shared, down)
+
+
+def rows_kernel(inner_ref, gate_ref, up_ref, out_ref, acc_ref):
+    step = pl.program_id(0)
+    product = dot_nn(inner_ref[0], gate_ref[0]) + dot_nn(inner_ref[1], up_ref[0])
+
+    @pl.when(step == 0)
+    def _():
+        acc_ref[...] = product
+
+    @pl.when((step > 0) & (step < pl.num_programs(0) - 1))
+    def _():
+        acc_ref[...] += product
+
+    @pl.when(step == pl.num_programs(0) - 1)
+    def _():
+        out_ref[...] = (acc_ref[...] + product).astype(BF16).reshape(out_ref.shape)
+
+
+def row_grads(inner, gate, up, capacity):
+    _, rows, units = inner.shape
+    width = gate.shape[2]
+    block = 256
+    weight = pl.BlockSpec((1, block, width), lambda i: (0, i, 0))
+    shape = (rows // capacity, capacity, width)
+    return pl.pallas_call(
+        rows_kernel,
+        grid=(units // block,),
+        in_specs=[pl.BlockSpec((2, rows, block), lambda i: (0, 0, i)), weight, weight],
+        out_specs=pl.BlockSpec(shape, lambda i: (0, 0, 0)),
+        out_shape=jax.ShapeDtypeStruct(shape, BF16),
+        scratch_shapes=[pltpu.VMEM((rows, width), F32)],
+        compiler_params=params(),
+        cost_estimate=cost(
+            4 * rows * units * width, 4 * units * width + 2 * rows * (width + 2 * units)
+        ),
+        name="grad_rows",
+    )(inner, gate, up)
+
+
+def mix_kernel(mix_ref, home_ref, out_ref):
+    for start in range(0, home_ref.shape[2], 512):
+        lanes = slice(start, start + 512)
+        home = home_ref[:, :, lanes].reshape(mix_ref.shape[1], 512)
+        out_ref[0, :, lanes] = dot_nn(mix_ref[...], home).astype(BF16)
+
+
+def mixed(mix, home):
+    tokens, slots = mix.shape
+    width = home.shape[2]
+    return pl.pallas_call(
+        mix_kernel,
+        out_shape=jax.ShapeDtypeStruct((1, tokens, width), BF16),
+        compiler_params=params(),
+        cost_estimate=cost(2 * slots * tokens * width, 2 * (slots + tokens) * width),
+        name="mixture",
+    )(mix, home)
+
+
+def partial_kernel(inner_ref, x_ref, grad_out_ref, out_ref):
+    def product(right):
+        return lax.dot_general(
+            inner_ref[0], right, (((0,), (0,)), ((), ())), preferred_element_type=F32
+        ).astype(BF16)
+
+    @pl.when(pl.program_id(0) < 2)
+    def _():
+        out_ref[...] = product(flat_rows(x_ref))
+
+    @pl.when(pl.program_id(0) == 2)
+    def _():
+        out_ref[...] = product(flat_rows(grad_out_ref))
+
+
+def partials(inner, x, shared):
+    kinds, rows, units = inner.shape
+    width = x.shape[2]
+    block = 256
+    count = units // block
+    whole = pl.BlockSpec(x.shape, lambda k, i: (0, 0, 0))
+    return pl.pallas_call(
+        partial_kernel,
+        grid=(kinds, count),
+        in_specs=[pl.BlockSpec((1, rows, block), lambda k, i: (k, 0, i)), whole, whole],
+        out_specs=pl.BlockSpec((block, width), lambda k, i: (k * count + i, 0)),
+        out_shape=jax.ShapeDtypeStruct((kinds * units, width), BF16),
+        compiler_params=pltpu.CompilerParams(vmem_limit_bytes=58 * 1024 * 1024),
+        cost_estimate=cost(2 * kinds * rows * units * width, 4 * (kinds * units + rows) * width),
+        name="partials",
+    )(inner, x, shared)
+
+
+def widen_kernel(in_ref, *out_refs):
+    units = out_refs[0].shape[1]
+    for k, out_ref in enumerate(out_refs):
+        out_ref[0] = in_ref[k * units : (k + 1) * units].astype(F32)
+
+
+def widen(grads, units):
+    rows, width = grads.shape
+    return pl.pallas_call(
+        widen_kernel,
+        out_shape=(jax.ShapeDtypeStruct((1, units, width), F32),) * (rows // units),
+        compiler_params=params(),
+        cost_estimate=cost(0, 6 * rows * width),
+        name="widen",
+    )(grads)
 
 
 def finish_kernel(take_ref, home_ref, stream_ref, inverse_ref, gain_ref, out_ref):
@@ -262,7 +434,8 @@
     total = 0.0
     for start in range(0, width, 512):
         lanes = slice(start, start + 512)
-        scaled = dot_nn(take_ref[...], home_ref[:, lanes]) * gain_ref[:, lanes]
+        home = home_ref[:, :, lanes].reshape(take_ref.shape[1], 512)
+        scaled = dot_nn(take_ref[...], home) * gain_ref[:, lanes]
         out_ref[0, :, lanes] = scaled
         total = total + jnp.sum(stream_ref[:, lanes] * scaled, axis=1, keepdims=True)
     factor = inverse * inverse * inverse * (total / width)
@@ -271,7 +444,7 @@
 
 def finish(take, home, stream, inverse, gain):
     tokens, width = stream.shape
-    slots = home.shape[0]
+    slots = take.shape[1]
     return pl.pallas_call(
         finish_kernel,
         out_shape=jax.ShapeDtypeStruct((1, tokens, width), F32),
@@ -279,6 +452,10 @@
         cost_estimate=cost(2 * slots * tokens * width, 2 * (slots + 4 * tokens) * width),
         name="finish",
     )(take, home, stream, inverse, gain)
+
+
+def in_hbm(values):
+    return pltpu.with_memory_space_constraint(values, pltpu.HBM)
 
 
 def swap(values, axis="expert"):
@@ -300,31 +477,28 @@
     up_full = lax.all_gather(w_up, "dp", axis=2, tiled=True)
 
     received = swap(pack(lengths, qkv, quarters))
-    put, take, mix, adjoint_send = route(expert_ids, gate_vals, cotangent, capacity, slots)
-    grad_out = swap(adjoint_send.reshape(owners, capacity, width)).reshape(slots, width)
-    att_home = swap(attend(received, head_size))
-    stream, inverse, normed_send = norm(lengths, att_home, resid, gain, put, quarters)
-    x_rows = swap(normed_send.reshape(owners, capacity, width)).reshape(slots, width)
-
-    grad_hidden = dot_nt(grad_out, down_full[0])
-    expert_out, hidden, grad_gate_pre, grad_up_pre = expert(
-        x_rows, grad_hidden, gate_full, up_full, down_full
+    put, take, mix, adjoint_send = route(
+        expert_ids, gate_vals, cotangent, capacity, slots, width // quarters
     )
-    out_home = swap(expert_out.reshape(owners, capacity, width)).reshape(slots, width)
-
-    def weight_grad(left, right):
-        part = lax.dot_general(left, right, (((0,), (0,)), ((), ())), preferred_element_type=F32)
-        return lax.psum_scatter(
-            part.astype(BF16)[None], "dp", scatter_dimension=2, tiled=True
-        ).astype(F32)
-
-    grad_gate = weight_grad(grad_gate_pre, x_rows)
-    grad_up = weight_grad(grad_up_pre, x_rows)
-    grad_down = weight_grad(hidden, grad_out)
-    grad_rows = (dot_nn(grad_gate_pre, gate_full[0]) + dot_nn(grad_up_pre, up_full[0])).astype(BF16)
-    grad_home = swap(grad_rows.reshape(owners, capacity, width)).reshape(slots, width)
-
-    mixture = dot_nn(mix, out_home).astype(BF16)[None]
+    shared = swap(in_hbm(attend(received, in_hbm(adjoint_send), head_size)))
+    stream, inverse, normed_send = norm(lengths, shared, resid, gain, put, quarters)
+    x_rows = swap(in_hbm(normed_send))
+
+    gate_full, up_full, down_full = in_hbm(gate_full), in_hbm(up_full), in_hbm(down_full)
+    grad_hidden = in_hbm(hidden_grad(shared, down_full))
+    expert_out, inner = expert(x_rows, grad_hidden, gate_full, up_full, down_full)
+    inner = in_hbm(inner)
+    out_home = swap(in_hbm(expert_out))
+
+    grads = lax.psum_scatter(
+        partials(inner, x_rows, shared), "dp", scatter_dimension=1, tiled=True
+    )
+    grad_gate, grad_up, grad_down = widen(grads, w_gate.shape[1])
+    grad_rows = in_hbm(row_grads(inner, gate_full, up_full, capacity))
+    grad_rows, out_home = lax.optimization_barrier((grad_rows, out_home))
+    grad_home = swap(grad_rows)
+
+    mixture = mixed(mix, out_home)
     grad_stream = finish(take, grad_home, stream, inverse, gain)
     return (mixture, grad_stream, grad_gate, grad_up, grad_down)
 

time: 358 us -> 338 us (0.944)
  Pallas kernels: 22.4 us -> 56.7 us
  matrix products: 30.6 us -> 0 us
  local copies, waits for them, and re-layouts: 13.1 us -> 6.98 us
  waiting for transfers between devices: 229 us -> 223 us
  other arithmetic: 5.79 us -> 0 us
  starting transfers between devices: 40.6 us -> 36.2 us
    pallas_call x1 -> x6, Pallas kernels: 0.99 us -> 32.2 us  [the longest x1 11.8 us: partials(): pl.pallas_call(partial_kernel, grid=(kinds, count), in_specs=[pl.BlockSpe...]
    dot_general x7 -> x0, matrix products: 30.6 us -> none  [the longest x3 15.1 us: weight_grad(): lax.dot_general(left, right, (((0,), (0,)), ((), ())), preferred_element_...]
    all_to_all x6 -> x5, waiting for transfers between devices: 227 us -> 221 us  [swap(): return lax.all_to_all(values, axis, split_axis=0, concat_axis=0, tiled=True)]
    unnamed x36 -> x22, local copies, waits for them, and re-layouts: 13.1 us -> 6.98 us
    convert_element_type x3 -> x0, other arithmetic: 5.79 us -> none  [weight_grad(): return lax.psum_scatter(part.astype(BF16)[None], 'dp', scatter_dimension=...]
    all_to_all x6 -> x5, starting transfers between devices: 39.9 us -> 35.8 us  [swap(): return lax.all_to_all(values, axis, split_axis=0, concat_axis=0, tiled=True)]
  transfers between devices with their start and end apart: 12 -> 9, of which waited for: 6 -> 5; matrix products, arithmetic and copies ran while one was open for 8% -> 0% of each run, Pallas kernels for 4% -> 9%
where the time goes in v1:
time: 338 us; the launch traced here: 337 us
  waiting for transfers between devices  223 us (66%)
  Pallas kernels  56.7 us (17%)
  starting transfers between devices  36.2 us (11%)
  between operations  14.5 us (4%)
  local copies, waits for them, and re-layouts  6.98 us (2%)
    all_to_all x5, waiting for transfers between devices, swap(): return lax.all_to_all(values, axis, split_axis=0, concat_axis=0, tiled=True)  221 us
    all_to_all x5, starting transfers between devices, swap(): return lax.all_to_all(values, axis, split_axis=0, concat_axis=0, tiled=True)  35.8 us
    pallas_call x1, Pallas kernels, partials(): pl.pallas_call(partial_kernel, grid=(kinds, count), in_specs=[pl.BlockSpe...  11.8 us
    pallas_call x1, Pallas kernels, expert(): pl.pallas_call(expert_kernel, grid=(units // block,), in_specs=[whole, co...  11.5 us
    pallas_call x1, Pallas kernels, row_grads(): pl.pallas_call(rows_kernel, grid=(units // block,), in_specs=[pl.BlockSpe...  8.03 us
    unnamed x22, local copies, waits for them, and re-layouts  6.98 us
    pallas_call x1, Pallas kernels, attend(): pl.pallas_call(functools.partial(attend_kernel, head_size, 1.0 / math.sqr...  6.89 us
  transfers between devices with their start and end apart: 9, of which 5 were waited for; matrix products, arithmetic and copies ran while one was open for 0% of the time, Pallas kernels for 9%

profile of v1, /device:TPU:16, one launch (start us, length us, event | category | flops | bytes accessed | tf_op | source)
XLA Modules:
  0.0 337.2 jit_solution(16449414279969948102)
XLA Ops:
  7.2 0.7 all-gather.4.cloned.1.call-update
  8.6 1.4 copy-done.2
  10.0 1.7 pack_qkv.1
  11.7 11.4 %all-to-all-start = ((bf16[32,3,16,512]{3,2,1,0:T(8,128)(2,1)}), bf16[32,3,16,512]{3,2,1,0:T(8,128)(2,1)S(1)}, u32[]{:S(2)}, u32[]{:S(2)}) async-start(bf16[32,3,16,512]{3,2,1,0:T(8,128)(2,1)} %pack_qkv.1), calls=%async_computation | async-start | bytes 3145728 | tf_op jit(solution)/shard_map/all_to_all | solution.py:462
  23.2 0.7 all-gather.6.cloned.1.call-update
  23.9 0.1 copy.17.gates_ref
  24.0 0.1 copy.16.ids_ref
  24.1 1.2 route.1
  25.3 1.5 copy-done
  26.8 35.4 %all-to-all-done.in_ref = bf16[32,3,16,512]{3,2,1,0:T(8,128)(2,1)S(1)} async-done(((bf16[32,3,16,512]{3,2,1,0:T(8,128)(2,1)}), bf16[32,3,16,512]{3,2,1,0:T(8,128)(2,1)S(1)}, u32[]{:S(2)}, u32[]{:S(2)}) %all-to-all-start) | async-done | bytes 1572896 | tf_op jit(solution)/shard_map/all_to_all | solution.py:462
  62.2 6.9 %attend.1 = bf16[32,16,2560]{2,1,0:T(8,128)(2,1)} custom-call(bf16[32,3,16,512]{3,2,1,0:T(8,128)(2,1)S(1)} %all-to-all-done.in_ref, bf16[32,16,2560]{2,1,0:T(8,128)(2,1)} %copy-done), custom_call_target="tpu_custom_call", output_to_operand_aliasing={{}: (1, {})} | custom-call | flops 536870912 | bytes 2097152 | tf_op jit(solution)/shard_map/attend/pallas_call | solution.py:107
  69.1 6.0 %all-to-all-start.1 = ((bf16[32,16,2560]{2,1,0:T(8,128)(2,1)}), bf16[32,16,2560]{2,1,0:T(8,128)(2,1)}, u32[]{:S(2)}, u32[]{:S(2)}) async-start(bf16[32,16,2560]{2,1,0:T(8,128)(2,1)} %attend.1), calls=%async_computation.1 | async-start | bytes 5242880 | tf_op jit(solution)/shard_map/all_to_all | solution.py:462
  75.2 0.7 all-gather.8.cloned.1.call-update
  75.9 59.3 %all-to-all-done.1.att_ref.grad_out_ref = bf16[32,16,2560]{2,1,0:T(8,128)(2,1)} async-done(((bf16[32,16,2560]{2,1,0:T(8,128)(2,1)}), bf16[32,16,2560]{2,1,0:T(8,128)(2,1)}, u32[]{:S(2)}, u32[]{:S(2)}) %all-to-all-start.1) | async-done | bytes 2621472 | tf_op jit(solution)/shard_map/all_to_all | solution.py:462
  135.1 3.3 norm.1
  138.5 6.2 %all-to-all-start.2 = ((bf16[32,16,2048]{2,1,0:T(8,128)(2,1)}), bf16[32,16,2048]{2,1,0:T(8,128)(2,1)}, u32[]{:S(2)}, u32[]{:S(2)}) async-start(bf16[32,16,2048]{2,1,0:T(8,128)(2,1)} %get-tuple-element.22), calls=%async_computation.2 | async-start | bytes 4194304 | tf_op jit(solution)/shard_map/all_to_all | solution.py:462
  144.7 0.2 reduce-scatter.2.cloned.1.call-start
  145.0 4.7 %grad_hidden.1.gh_ref = f32[512,768]{1,0:T(8,128)S(1)} custom-call(bf16[32,16,2560]{2,1,0:T(8,128)(2,1)} %all-to-all-done.1.att_ref.grad_out_ref, bf16[1,768,2048]{2,1,0:T(8,128)(2,1)} %all-gather.4.cloned.1.call-done.down_ref), custom_call_target="tpu_custom_call" | custom-call | flops 1610612736 | bytes 6815744 | tf_op jit(solution)/shard_map/grad_hidden/pallas_call | solution.py:309
  149.7 1.2 copy-done.1
  150.9 42.0 %all-to-all-done.2.x_ref = bf16[32,16,2048]{2,1,0:T(8,128)(2,1)} async-done(((bf16[32,16,2048]{2,1,0:T(8,128)(2,1)}), bf16[32,16,2048]{2,1,0:T(8,128)(2,1)}, u32[]{:S(2)}, u32[]{:S(2)}) %all-to-all-start.2) | async-done | bytes 2097184 | tf_op jit(solution)/shard_map/all_to_all | solution.py:462
  192.8 11.5 %expert.1 = (bf16[32,16,2048]{2,1,0:T(8,128)(2,1)}, bf16[3,512,768]{2,1,0:T(8,128)(2,1)S(1)}) custom-call(bf16[32,16,2048]{2,1,0:T(8,128)(2,1)} %all-to-all-done.2.x_ref, f32[512,768]{1,0:T(8,128)} %copy-done.1, bf16[1,768,2048]{2,1,0:T(8,128)(2,1)} %all-gather.6.cloned.1.call-done.gate_ref, bf16[1,768,2048]{2,1,0:T(8,128)(2,1)} %all-gather.8.cloned.1.call-done.up_ref, ...), custom_call_target="tpu_custom_call" | custom-call | flops 4831838208 | bytes 13631488 | tf_op jit(solution)/shard_map/expert/pallas_call | solution.py:280
  204.3 1.4 copy-done.7
  205.7 11.8 %partials.1 = bf16[2304,2048]{1,0:T(8,128)(2,1)} custom-call(bf16[3,512,768]{2,1,0:T(8,128)(2,1)} %copy-done.7, bf16[32,16,2048]{2,1,0:T(8,128)(2,1)} %all-to-all-done.2.x_ref, bf16[32,16,2560]{2,1,0:T(8,128)(2,1)} %all-to-all-done.1.att_ref.grad_out_ref), custom_call_target="tpu_custom_call" | custom-call | flops 4831838208 | bytes 23068672 | tf_op jit(solution)/shard_map/partials/pallas_call | solution.py:402
  217.6 6.1 %all-to-all-start.3 = ((bf16[32,16,2048]{2,1,0:T(8,128)(2,1)}), bf16[32,16,2048]{2,1,0:T(8,128)(2,1)}, u32[]{:S(2)}, u32[]{:S(2)}) async-start(bf16[32,16,2048]{2,1,0:T(8,128)(2,1)} %get-tuple-element.24), calls=%async_computation.3 | async-start | bytes 4194304 | tf_op jit(solution)/shard_map/all_to_all | solution.py:462
  223.6 8.0 %grad_rows.1 = bf16[32,16,2048]{2,1,0:T(8,128)(2,1)} custom-call(bf16[3,512,768]{2,1,0:T(8,128)(2,1)} %copy-done.7, bf16[1,768,2048]{2,1,0:T(8,128)(2,1)} %all-gather.6.cloned.1.call-done.gate_ref, bf16[1,768,2048]{2,1,0:T(8,128)(2,1)} %all-gather.8.cloned.1.call-done.up_ref), custom_call_target="tpu_custom_call" | custom-call | flops 3221225472 | bytes 9961472 | tf_op jit(solution)/shard_map/grad_rows/pallas_call | solution.py:347
  231.7 39.5 %all-to-all-done.3.home_ref = bf16[32,16,2048]{2,1,0:T(8,128)(2,1)} async-done(((bf16[32,16,2048]{2,1,0:T(8,128)(2,1)}), bf16[32,16,2048]{2,1,0:T(8,128)(2,1)}, u32[]{:S(2)}, u32[]{:S(2)}) %all-to-all-start.3) | async-done | bytes 2097184 | tf_op jit(solution)/shard_map/all_to_all | solution.py:462
  271.1 6.1 %all-to-all-start.4 = ((bf16[32,16,2048]{2,1,0:T(8,128)(2,1)}), bf16[32,16,2048]{2,1,0:T(8,128)(2,1)}, u32[]{:S(2)}, u32[]{:S(2)}) async-start(bf16[32,16,2048]{2,1,0:T(8,128)(2,1)} %grad_rows.1), calls=%async_computation.4 | async-start | bytes 4194304 | tf_op jit(solution)/shard_map/all_to_all | solution.py:462
  277.2 2.8 mixture.1
  280.1 44.5 %all-to-all-done.4.home_ref = bf16[32,16,2048]{2,1,0:T(8,128)(2,1)} async-done(((bf16[32,16,2048]{2,1,0:T(8,128)(2,1)}), bf16[32,16,2048]{2,1,0:T(8,128)(2,1)}, u32[]{:S(2)}, u32[]{:S(2)}) %all-to-all-start.4) | async-done | bytes 2097184 | tf_op jit(solution)/shard_map/all_to_all | solution.py:462
  324.6 3.3 finish.1
  327.9 1.3 copy-done.3
  329.1 1.5 widen.1
  (23 shorter events, 0.2 us)
Async XLA Ops:
  7.2 137.8 %all-gather.4.cloned.1.call-start = ((), (), s32[]{:S(2)}) async-start(), calls=%async_computation.6 | async-start | bytes 3538944 | tf_op jit(solution)/shard_map/all_gather | solution.py:475
  8.5 1.4 copy-start.2
  11.7 12.2 %copy-start.9 = (bf16[1,128,2]{1,2,0:T(2,128)(2,1)S(1)}, bf16[1,128,2]{1,2,0:T(2,128)(2,1)}, u32[]{:S(2)}) copy-start(bf16[1,128,2]{1,2,0:T(2,128)(2,1)} %param.15) | copy-start | bytes 1540
  11.7 12.4 %copy-start.8 = (s32[1,128,2]{1,2,0:T(2,128)S(1)}, s32[1,128,2]{1,2,0:T(2,128)}, u32[]{:S(2)}) copy-start(s32[1,128,2]{1,2,0:T(2,128)} %param.14) | copy-start | bytes 3076
  11.7 12.5 %copy-start.6 = (bf16[1,128,2048]{2,1,0:T(8,128)(2,1)S(1)}, bf16[1,128,2048]{2,1,0:T(8,128)(2,1)}, u32[]{:S(2)}) copy-start(bf16[1,128,2048]{2,1,0:T(8,128)(2,1)} %cotangent_ref.1) | copy-start | bytes 1572868
  11.7 50.6 %all-to-all-start = ((bf16[32,3,16,512]{3,2,1,0:T(8,128)(2,1)}), bf16[32,3,16,512]{3,2,1,0:T(8,128)(2,1)S(1)}, u32[]{:S(2)}, u32[]{:S(2)}) async-start(bf16[32,3,16,512]{3,2,1,0:T(8,128)(2,1)} %pack_qkv.1), calls=%async_computation | async-start | bytes 3145728 | tf_op jit(solution)/shard_map/all_to_all | solution.py:462
  23.1 127.7 %all-gather.6.cloned.1.call-start = ((), (), s32[]{:S(2)}) async-start(), calls=%async_computation.7 | async-start | bytes 3538944 | tf_op jit(solution)/shard_map/all_gather | solution.py:476
  25.3 1.5 copy-start
  69.1 66.0 %copy-start.4 = (bf16[1,128,2048]{2,1,0:T(8,128)(2,1)S(1)}, bf16[1,128,2048]{2,1,0:T(8,128)(2,1)}, u32[]{:S(2)}) copy-start(bf16[1,128,2048]{2,1,0:T(8,128)(2,1)} %resid_ref.1) | copy-start | bytes 1572868
  69.1 66.0 %copy-start.5 = (f32[2048]{0:T(1024)S(1)}, f32[2048]{0:T(1024)}, u32[]{:S(2)}) copy-start(f32[2048]{0:T(1024)} %param.13) | copy-start | bytes 24580
  69.1 66.0 %all-to-all-start.1 = ((bf16[32,16,2560]{2,1,0:T(8,128)(2,1)}), bf16[32,16,2560]{2,1,0:T(8,128)(2,1)}, u32[]{:S(2)}, u32[]{:S(2)}) async-start(bf16[32,16,2560]{2,1,0:T(8,128)(2,1)} %attend.1), calls=%async_computation.1 | async-start | bytes 5242880 | tf_op jit(solution)/shard_map/all_to_all | solution.py:462
  75.1 75.7 %all-gather.8.cloned.1.call-start = ((), (), s32[]{:S(2)}) async-start(), calls=%async_computation.8 | async-start | bytes 3538944 | tf_op jit(solution)/shard_map/all_gather | solution.py:477
  138.5 54.4 %all-to-all-start.2 = ((bf16[32,16,2048]{2,1,0:T(8,128)(2,1)}), bf16[32,16,2048]{2,1,0:T(8,128)(2,1)}, u32[]{:S(2)}, u32[]{:S(2)}) async-start(bf16[32,16,2048]{2,1,0:T(8,128)(2,1)} %get-tuple-element.22), calls=%async_computation.2 | async-start | bytes 4194304 | tf_op jit(solution)/shard_map/all_to_all | solution.py:462
  144.7 183.1 %reduce-scatter.2.cloned.1.call-start = ((), (), s32[]{:S(2)}) async-start(), calls=%async_computation.9 | async-start | bytes 10616832 | tf_op jit(solution)/shard_map/reduce_scatter | solution.py:493
  149.7 1.2 copy-start.1
  204.3 1.4 copy-start.7
  217.6 53.6 %all-to-all-start.3 = ((bf16[32,16,2048]{2,1,0:T(8,128)(2,1)}), bf16[32,16,2048]{2,1,0:T(8,128)(2,1)}, u32[]{:S(2)}, u32[]{:S(2)}) async-start(bf16[32,16,2048]{2,1,0:T(8,128)(2,1)} %get-tuple-element.24), calls=%async_computation.3 | async-start | bytes 4194304 | tf_op jit(solution)/shard_map/all_to_all | solution.py:462
  271.1 53.5 %all-to-all-start.4 = ((bf16[32,16,2048]{2,1,0:T(8,128)(2,1)}), bf16[32,16,2048]{2,1,0:T(8,128)(2,1)}, u32[]{:S(2)}, u32[]{:S(2)}) async-start(bf16[32,16,2048]{2,1,0:T(8,128)(2,1)} %grad_rows.1), calls=%async_computation.4 | async-start | bytes 4194304 | tf_op jit(solution)/shard_map/all_to_all | solution.py:462
  327.9 1.3 copy-start.3
Sparse Core Ops, SparseCore 0:
  9.8 36.6 all-gather.3
  48.4 35.2 all-gather.5
  85.5 35.2 all-gather.7
  217.7 55.1 reduce-scatter.1

commit v2 on v1

--- a/solution.py
+++ b/solution.py
@@ -12,7 +12,7 @@
 ABSENT = 100.0
 F32 = jnp.float32
 BF16 = jnp.bfloat16
-VMEM_LIMIT = 40 * 1024 * 1024
+LONG = 10**15
 
 
 def cost(flops, bytes_accessed, transcendentals=0):
@@ -21,8 +21,8 @@
     )
 
 
-def params():
-    return pltpu.CompilerParams(vmem_limit_bytes=VMEM_LIMIT)
+def params(mebibytes=40):
+    return pltpu.CompilerParams(vmem_limit_bytes=mebibytes * 1024 * 1024)
 
 
 def dot_nt(a, b):
@@ -72,30 +72,31 @@
     )(lengths, qkv)
 
 
-def attend_kernel(head_size, scale, in_ref, shared_ref, out_ref):
+def attend_kernel(head_size, scale, in_ref, shared_ref, out_ref, bias_ref):
     del shared_ref
     series, _, times, wide = in_ref.shape
     pairs = series * times
     chunk = 128
-    for head in range(wide // head_size):
-        lanes = slice(head * head_size, (head + 1) * head_size)
-        keys = in_ref[:, 1, :, lanes].reshape(pairs, head_size)
-        values = in_ref[:, 2, :, lanes].reshape(pairs, head_size)
-        total = dot_nt(jnp.ones((8, head_size), BF16), keys)[0:1]
-        live = total < 0.5 * ABSENT * head_size
-        for part in range(pairs // chunk):
-            first = part * chunk // times
-            count = chunk // times
+    keys = in_ref[:, 1, :, 0:head_size].reshape(pairs, head_size)
+    total = dot_nt(jnp.ones((8, head_size), BF16), keys)[0:1]
+    live = total < 0.5 * ABSENT * head_size
+    for part in range(pairs // chunk):
+        first = part * chunk // times
+        count = chunk // times
+        row = part * chunk + lax.broadcasted_iota(jnp.int32, (chunk, pairs), 0)
+        column = lax.broadcasted_iota(jnp.int32, (chunk, pairs), 1)
+        allowed = (((row ^ column) & (times - 1)) == 0) & (live | (row == column))
+        bias_ref[...] = jnp.where(allowed, 0.0, -1e30)
+        for head in range(wide // head_size):
+            lanes = slice(head * head_size, (head + 1) * head_size)
             queries = in_ref[first : first + count, 0, :, lanes].reshape(chunk, head_size)
-            scores = dot_nt(queries, keys) * scale
-            row = part * chunk + lax.broadcasted_iota(jnp.int32, (chunk, pairs), 0)
-            column = lax.broadcasted_iota(jnp.int32, (chunk, pairs), 1)
-            allowed = (((row ^ column) & (times - 1)) == 0) & (live | (row == column))
-            scores = jnp.where(allowed, scores, -1e30)
+            keys = in_ref[:, 1, :, lanes].reshape(pairs, head_size)
+            values = in_ref[:, 2, :, lanes].reshape(pairs, head_size)
+            scores = dot_nt(queries, keys) * scale + bias_ref[...]
             highest = jnp.max(scores, axis=1, keepdims=True)
-            raised = jnp.exp(scores - highest)
-            weights = (raised / jnp.sum(raised, axis=1, keepdims=True)).astype(BF16)
-            attended = dot_nn(weights, values).astype(BF16)
+            raised = jnp.exp2(scores - highest).astype(BF16)
+            both = dot_nn(raised, jnp.concatenate([values, jnp.ones_like(values)], axis=1))
+            attended = (both[:, :head_size] / both[:, head_size:]).astype(BF16)
             out_ref[first : first + count, :, lanes] = attended.reshape(count, times, head_size)
 
 
@@ -105,7 +106,7 @@
     heads = wide // head_size
     last = shared.shape[2] // wide - 1
     return pl.pallas_call(
-        functools.partial(attend_kernel, head_size, 1.0 / math.sqrt(head_size)),
+        functools.partial(attend_kernel, head_size, math.log2(math.e) / math.sqrt(head_size)),
         grid=(1,),
         in_specs=[
             pl.BlockSpec(received.shape, lambda i: (0, 0, 0, 0)),
@@ -114,6 +115,7 @@
         out_specs=pl.BlockSpec((series, times, wide), lambda i: (0, 0, last)),
         out_shape=jax.ShapeDtypeStruct(shared.shape, BF16),
         input_output_aliases={1: 0},
+        scratch_shapes=[pltpu.VMEM((128, pairs), F32)],
         compiler_params=params(),
         cost_estimate=cost(
             4 * heads * pairs * pairs * head_size, received.size * 8 // 3, heads * pairs * pairs
@@ -287,9 +289,7 @@
             jax.ShapeDtypeStruct((3, rows, units), BF16),
         ),
         scratch_shapes=[pltpu.VMEM((rows, width), F32)],
-        compiler_params=pltpu.CompilerParams(
-            dimension_semantics=("arbitrary",), vmem_limit_bytes=VMEM_LIMIT
-        ),
+        compiler_params=params(60),
         cost_estimate=cost(
             6 * rows * width * units, 4 * rows * width + 6 * units * width, rows * units
         ),
@@ -373,7 +373,7 @@
         mix_kernel,
         out_shape=jax.ShapeDtypeStruct((1, tokens, width), BF16),
         compiler_params=params(),
-        cost_estimate=cost(2 * slots * tokens * width, 2 * (slots + tokens) * width),
+        cost_estimate=cost(LONG, LONG // 1000),
         name="mixture",
     )(mix, home)
 
@@ -405,7 +405,7 @@
         in_specs=[pl.BlockSpec((1, rows, block), lambda k, i: (k, 0, i)), whole, whole],
         out_specs=pl.BlockSpec((block, width), lambda k, i: (k * count + i, 0)),
         out_shape=jax.ShapeDtypeStruct((kinds * units, width), BF16),
-        compiler_params=pltpu.CompilerParams(vmem_limit_bytes=58 * 1024 * 1024),
+        compiler_params=params(58),
         cost_estimate=cost(2 * kinds * rows * units * width, 4 * (kinds * units + rows) * width),
         name="partials",
     )(inner, x, shared)
@@ -487,7 +487,6 @@
     gate_full, up_full, down_full = in_hbm(gate_full), in_hbm(up_full), in_hbm(down_full)
     grad_hidden = in_hbm(hidden_grad(shared, down_full))
     expert_out, inner = expert(x_rows, grad_hidden, gate_full, up_full, down_full)
-    inner = in_hbm(inner)
     out_home = swap(in_hbm(expert_out))
 
     grads = lax.psum_scatter(
@@ -499,6 +498,7 @@
     grad_home = swap(grad_rows)
 
     mixture = mixed(mix, out_home)
+    take, grad_gate = lax.optimization_barrier((take, grad_gate))
     grad_stream = finish(take, grad_home, stream, inverse, gain)
     return (mixture, grad_stream, grad_gate, grad_up, grad_down)
 

time: 338 us -> 318 us (0.941)
  waiting for transfers between devices: 223 us -> 207 us
  Pallas kernels: 56.7 us -> 52.6 us
    all_to_all x5, waiting for transfers between devices: 221 us -> 190 us  [swap(): return lax.all_to_all(values, axis, split_axis=0, concat_axis=0, tiled=True)]
    reduce_scatter x1, waiting for transfers between devices: 0.01 us -> 14.8 us  [body(): lax.psum_scatter(partials(inner, x_rows, shared), 'dp', scatter_dimension...]
    pallas_call x1, Pallas kernels: 6.89 us -> 2.48 us  [attend(): pl.pallas_call(functools.partial(attend_kernel, head_size, math.log2(math...]
  transfers between devices with their start and end apart: 9 -> 9, of which waited for: 5 -> 6; matrix products, arithmetic and copies ran while one was open for 0% -> 0% of each run, Pallas kernels for 9% -> 12%
where the time goes in v2:
time: 318 us; the launch traced here: 317 us
  waiting for transfers between devices  207 us (65%)
  Pallas kernels  52.6 us (17%)
  starting transfers between devices  36.2 us (11%)
  between operations  14.5 us (5%)
  local copies, waits for them, and re-layouts  7.21 us (2%)
    all_to_all x5, waiting for transfers between devices, swap(): return lax.all_to_all(values, axis, split_axis=0, concat_axis=0, tiled=True)  190 us
    all_to_all x5, starting transfers between devices, swap(): return lax.all_to_all(values, axis, split_axis=0, concat_axis=0, tiled=True)  35.8 us
    reduce_scatter x1, waiting for transfers between devices, body(): lax.psum_scatter(partials(inner, x_rows, shared), 'dp', scatter_dimension...  14.8 us
    pallas_call x1, Pallas kernels, expert(): pl.pallas_call(expert_kernel, grid=(units // block,), in_specs=[whole, co...  11.9 us
    pallas_call x1, Pallas kernels, partials(): pl.pallas_call(partial_kernel, grid=(kinds, count), in_specs=[pl.BlockSpe...  11.9 us
    pallas_call x1, Pallas kernels, row_grads(): pl.pallas_call(rows_kernel, grid=(units // block,), in_specs=[pl.BlockSpe...  7.72 us
    unnamed x22, local copies, waits for them, and re-layouts  7.21 us
  transfers between devices with their start and end apart: 9, of which 6 were waited for; matrix products, arithmetic and copies ran while one was open for 0% of the time, Pallas kernels for 12%

profile of v2, /device:TPU:16, one launch (start us, length us, event | category | flops | bytes accessed | tf_op | source)
XLA Modules:
  0.0 317.2 jit_solution(4630806743534641933)
XLA Ops:
  7.2 0.7 all-gather.4.cloned.1.call-update
  8.6 1.4 copy-done.2
  10.0 1.7 pack_qkv.1
  11.7 11.4 %all-to-all-start = ((bf16[32,3,16,512]{3,2,1,0:T(8,128)(2,1)}), bf16[32,3,16,512]{3,2,1,0:T(8,128)(2,1)S(1)}, u32[]{:S(2)}, u32[]{:S(2)}) async-start(bf16[32,3,16,512]{3,2,1,0:T(8,128)(2,1)} %pack_qkv.1), calls=%async_computation | async-start | bytes 3145728 | tf_op jit(solution)/shard_map/all_to_all | solution.py:462
  23.2 0.7 all-gather.6.cloned.1.call-update
  23.9 0.1 copy.17.gates_ref
  24.1 1.2 route.1
  25.3 1.5 copy-done
  26.8 35.4 %all-to-all-done.in_ref = bf16[32,3,16,512]{3,2,1,0:T(8,128)(2,1)S(1)} async-done(((bf16[32,3,16,512]{3,2,1,0:T(8,128)(2,1)}), bf16[32,3,16,512]{3,2,1,0:T(8,128)(2,1)S(1)}, u32[]{:S(2)}, u32[]{:S(2)}) %all-to-all-start) | async-done | bytes 1572896 | tf_op jit(solution)/shard_map/all_to_all | solution.py:462
  62.2 2.5 attend.1
  64.7 6.0 %all-to-all-start.1 = ((bf16[32,16,2560]{2,1,0:T(8,128)(2,1)}), bf16[32,16,2560]{2,1,0:T(8,128)(2,1)}, u32[]{:S(2)}, u32[]{:S(2)}) async-start(bf16[32,16,2560]{2,1,0:T(8,128)(2,1)} %attend.1), calls=%async_computation.1 | async-start | bytes 5242880 | tf_op jit(solution)/shard_map/all_to_all | solution.py:462
  70.8 0.7 all-gather.8.cloned.1.call-update
  71.5 59.3 %all-to-all-done.1.att_ref.grad_out_ref = bf16[32,16,2560]{2,1,0:T(8,128)(2,1)} async-done(((bf16[32,16,2560]{2,1,0:T(8,128)(2,1)}), bf16[32,16,2560]{2,1,0:T(8,128)(2,1)}, u32[]{:S(2)}, u32[]{:S(2)}) %all-to-all-start.1) | async-done | bytes 2621472 | tf_op jit(solution)/shard_map/all_to_all | solution.py:462
  130.7 3.4 %norm.1 = (f32[128,2048]{1,0:T(8,128)S(1)}, f32[128,128]{1,0:T(8,128)S(1)}, bf16[32,16,2048]{2,1,0:T(8,128)(2,1)}) custom-call(s32[1]{0:T(128)S(6)} %copy.19.lengths_ref, bf16[32,16,2560]{2,1,0:T(8,128)(2,1)} %all-to-all-done.1.att_ref.grad_out_ref, bf16[1,128,2048]{2,1,0:T(8,128)(2,1)S(1)} %copy-done.4, f32[1,2048]{1,0:T(1,128)S(1)} %bitcast.1, ...), custom_call_target="tpu_custom_call" | custom-call | flops 268435456 | bytes 4194304 | tf_op jit(solution)/shard_map/norm/pallas_call | solution.py:218
  134.1 6.2 %all-to-all-start.2 = ((bf16[32,16,2048]{2,1,0:T(8,128)(2,1)}), bf16[32,16,2048]{2,1,0:T(8,128)(2,1)}, u32[]{:S(2)}, u32[]{:S(2)}) async-start(bf16[32,16,2048]{2,1,0:T(8,128)(2,1)} %get-tuple-element.24), calls=%async_computation.2 | async-start | bytes 4194304 | tf_op jit(solution)/shard_map/all_to_all | solution.py:462
  140.4 4.7 %grad_hidden.1.gh_ref = f32[512,768]{1,0:T(8,128)S(1)} custom-call(bf16[32,16,2560]{2,1,0:T(8,128)(2,1)} %all-to-all-done.1.att_ref.grad_out_ref, bf16[1,768,2048]{2,1,0:T(8,128)(2,1)} %all-gather.4.cloned.1.call-done.down_ref), custom_call_target="tpu_custom_call" | custom-call | flops 1610612736 | bytes 6815744 | tf_op jit(solution)/shard_map/grad_hidden/pallas_call | solution.py:309
  145.1 1.1 copy-done.1
  146.3 42.2 %all-to-all-done.2.x_ref = bf16[32,16,2048]{2,1,0:T(8,128)(2,1)} async-done(((bf16[32,16,2048]{2,1,0:T(8,128)(2,1)}), bf16[32,16,2048]{2,1,0:T(8,128)(2,1)}, u32[]{:S(2)}, u32[]{:S(2)}) %all-to-all-start.2) | async-done | bytes 2097184 | tf_op jit(solution)/shard_map/all_to_all | solution.py:462
  188.5 11.9 %expert.1 = (bf16[32,16,2048]{2,1,0:T(8,128)(2,1)}, bf16[3,512,768]{2,1,0:T(8,128)(2,1)}) custom-call(bf16[32,16,2048]{2,1,0:T(8,128)(2,1)} %all-to-all-done.2.x_ref, f32[512,768]{1,0:T(8,128)} %copy-done.1, bf16[1,768,2048]{2,1,0:T(8,128)(2,1)} %all-gather.6.cloned.1.call-done.gate_ref, bf16[1,768,2048]{2,1,0:T(8,128)(2,1)} %all-gather.8.cloned.1.call-done.up_ref, ...), custom_call_target="tpu_custom_call" | custom-call | flops 4831838208 | bytes 13631488 | tf_op jit(solution)/shard_map/expert/pallas_call | solution.py:282
  200.3 6.1 %all-to-all-start.3 = ((bf16[32,16,2048]{2,1,0:T(8,128)(2,1)}), bf16[32,16,2048]{2,1,0:T(8,128)(2,1)}, u32[]{:S(2)}, u32[]{:S(2)}) async-start(bf16[32,16,2048]{2,1,0:T(8,128)(2,1)} %get-tuple-element.26), calls=%async_computation.3 | async-start | bytes 4194304 | tf_op jit(solution)/shard_map/all_to_all | solution.py:462
  206.4 0.2 reduce-scatter.2.cloned.1.call-start
  206.7 11.9 %partials.1 = bf16[2304,2048]{1,0:T(8,128)(2,1)} custom-call(bf16[3,512,768]{2,1,0:T(8,128)(2,1)} %get-tuple-element.25.inner_ref, bf16[32,16,2048]{2,1,0:T(8,128)(2,1)} %all-to-all-done.2.x_ref, bf16[32,16,2560]{2,1,0:T(8,128)(2,1)} %all-to-all-done.1.att_ref.grad_out_ref), custom_call_target="tpu_custom_call" | custom-call | flops 4831838208 | bytes 23068672 | tf_op jit(solution)/shard_map/partials/pallas_call | solution.py:402
  218.5 1.7 copy-done.7
  220.2 7.7 %grad_rows.1 = bf16[32,16,2048]{2,1,0:T(8,128)(2,1)} custom-call(bf16[3,512,768]{2,1,0:T(8,128)(2,1)S(1)} %copy-done.7, bf16[1,768,2048]{2,1,0:T(8,128)(2,1)} %all-gather.6.cloned.1.call-done.gate_ref, bf16[1,768,2048]{2,1,0:T(8,128)(2,1)} %all-gather.8.cloned.1.call-done.up_ref), custom_call_target="tpu_custom_call" | custom-call | flops 3221225472 | bytes 9961472 | tf_op jit(solution)/shard_map/grad_rows/pallas_call | solution.py:347
  227.9 26.0 %all-to-all-done.3.home_ref = bf16[32,16,2048]{2,1,0:T(8,128)(2,1)} async-done(((bf16[32,16,2048]{2,1,0:T(8,128)(2,1)}), bf16[32,16,2048]{2,1,0:T(8,128)(2,1)}, u32[]{:S(2)}, u32[]{:S(2)}) %all-to-all-start.3) | async-done | bytes 2097184 | tf_op jit(solution)/shard_map/all_to_all | solution.py:462
  253.9 6.1 %all-to-all-start.4 = ((bf16[32,16,2048]{2,1,0:T(8,128)(2,1)}), bf16[32,16,2048]{2,1,0:T(8,128)(2,1)}, u32[]{:S(2)}, u32[]{:S(2)}) async-start(bf16[32,16,2048]{2,1,0:T(8,128)(2,1)} %grad_rows.1), calls=%async_computation.5 | async-start | bytes 4194304 | tf_op jit(solution)/shard_map/all_to_all | solution.py:462
  260.0 2.9 mixture.1
  262.9 14.8 %reduce-scatter.2.cloned.1.call-done.in_ref = bf16[2304,256]{1,0:T(8,128)(2,1)} async-done(((bf16[2304,2048]{1,0:T(8,128)(2,1)}), bf16[2304,256]{1,0:T(8,128)(2,1)}) %reduce-scatter.2.cloned.1.call-update) | async-done | bytes 1179664 | tf_op jit(solution)/shard_map/reduce_scatter | solution.py:492
  277.7 1.3 copy-done.3
  278.9 1.5 widen.1
  280.4 26.9 %all-to-all-done.4.home_ref = bf16[32,16,2048]{2,1,0:T(8,128)(2,1)} async-done(((bf16[32,16,2048]{2,1,0:T(8,128)(2,1)}), bf16[32,16,2048]{2,1,0:T(8,128)(2,1)}, u32[]{:S(2)}, u32[]{:S(2)}) %all-to-all-start.4) | async-done | bytes 2097184 | tf_op jit(solution)/shard_map/all_to_all | solution.py:462
  307.4 3.3 %finish.1 = f32[1,128,2048]{2,1,0:T(8,128)} custom-call(bf16[128,512]{1,0:T(8,128)(2,1)S(1)} %get-tuple-element.30.take_ref, bf16[32,16,2048]{2,1,0:T(8,128)(2,1)} %all-to-all-done.4.home_ref, f32[128,2048]{1,0:T(8,128)S(1)} %get-tuple-element.32.stream_ref, f32[128,128]{1,0:T(8,128)S(1)} %get-tuple-element.33.inverse_ref, f32[1,2048]{1,0:T(1,128)S(1)} %bitcast.2), custom_call_target="tpu_custom_call" | custom-call | flops 268435456 | bytes 4194304 | tf_op jit(solution)/shard_map/finish/pallas_call | solution.py:448
  (23 shorter events, 0.3 us)
Async XLA Ops:
  7.2 133.2 %all-gather.4.cloned.1.call-start = ((), (), s32[]{:S(2)}) async-start(), calls=%async_computation.6 | async-start | bytes 3538944 | tf_op jit(solution)/shard_map/all_gather | solution.py:475
  8.5 1.4 copy-start.2
  11.7 12.2 %copy-start.9 = (bf16[1,128,2]{1,2,0:T(2,128)(2,1)S(1)}, bf16[1,128,2]{1,2,0:T(2,128)(2,1)}, u32[]{:S(2)}) copy-start(bf16[1,128,2]{1,2,0:T(2,128)(2,1)} %param.15) | copy-start | bytes 1540
  11.7 12.4 %copy-start.8 = (s32[1,128,2]{1,2,0:T(2,128)S(1)}, s32[1,128,2]{1,2,0:T(2,128)}, u32[]{:S(2)}) copy-start(s32[1,128,2]{1,2,0:T(2,128)} %param.14) | copy-start | bytes 3076
  11.7 12.5 %copy-start.6 = (bf16[1,128,2048]{2,1,0:T(8,128)(2,1)S(1)}, bf16[1,128,2048]{2,1,0:T(8,128)(2,1)}, u32[]{:S(2)}) copy-start(bf16[1,128,2048]{2,1,0:T(8,128)(2,1)} %cotangent_ref.1) | copy-start | bytes 1572868
  11.7 50.6 %all-to-all-start = ((bf16[32,3,16,512]{3,2,1,0:T(8,128)(2,1)}), bf16[32,3,16,512]{3,2,1,0:T(8,128)(2,1)S(1)}, u32[]{:S(2)}, u32[]{:S(2)}) async-start(bf16[32,3,16,512]{3,2,1,0:T(8,128)(2,1)} %pack_qkv.1), calls=%async_computation | async-start | bytes 3145728 | tf_op jit(solution)/shard_map/all_to_all | solution.py:462
  23.1 123.1 %all-gather.6.cloned.1.call-start = ((), (), s32[]{:S(2)}) async-start(), calls=%async_computation.7 | async-start | bytes 3538944 | tf_op jit(solution)/shard_map/all_gather | solution.py:476
  25.3 1.5 copy-start
  64.7 66.0 %copy-start.4 = (bf16[1,128,2048]{2,1,0:T(8,128)(2,1)S(1)}, bf16[1,128,2048]{2,1,0:T(8,128)(2,1)}, u32[]{:S(2)}) copy-start(bf16[1,128,2048]{2,1,0:T(8,128)(2,1)} %resid_ref.1) | copy-start | bytes 1572868
  64.7 66.0 %copy-start.5 = (f32[2048]{0:T(1024)S(1)}, f32[2048]{0:T(1024)}, u32[]{:S(2)}) copy-start(f32[2048]{0:T(1024)} %param.13) | copy-start | bytes 24580
  64.7 66.0 %all-to-all-start.1 = ((bf16[32,16,2560]{2,1,0:T(8,128)(2,1)}), bf16[32,16,2560]{2,1,0:T(8,128)(2,1)}, u32[]{:S(2)}, u32[]{:S(2)}) async-start(bf16[32,16,2560]{2,1,0:T(8,128)(2,1)} %attend.1), calls=%async_computation.1 | async-start | bytes 5242880 | tf_op jit(solution)/shard_map/all_to_all | solution.py:462
  70.7 75.5 %all-gather.8.cloned.1.call-start = ((), (), s32[]{:S(2)}) async-start(), calls=%async_computation.8 | async-start | bytes 3538944 | tf_op jit(solution)/shard_map/all_gather | solution.py:477
  134.1 54.4 %all-to-all-start.2 = ((bf16[32,16,2048]{2,1,0:T(8,128)(2,1)}), bf16[32,16,2048]{2,1,0:T(8,128)(2,1)}, u32[]{:S(2)}, u32[]{:S(2)}) async-start(bf16[32,16,2048]{2,1,0:T(8,128)(2,1)} %get-tuple-element.24), calls=%async_computation.2 | async-start | bytes 4194304 | tf_op jit(solution)/shard_map/all_to_all | solution.py:462
  145.1 1.1 copy-start.1
  200.3 53.6 %all-to-all-start.3 = ((bf16[32,16,2048]{2,1,0:T(8,128)(2,1)}), bf16[32,16,2048]{2,1,0:T(8,128)(2,1)}, u32[]{:S(2)}, u32[]{:S(2)}) async-start(bf16[32,16,2048]{2,1,0:T(8,128)(2,1)} %get-tuple-element.26), calls=%async_computation.3 | async-start | bytes 4194304 | tf_op jit(solution)/shard_map/all_to_all | solution.py:462
  206.4 71.2 %reduce-scatter.2.cloned.1.call-start = ((), (), s32[]{:S(2)}) async-start(), calls=%async_computation.9 | async-start | bytes 10616832 | tf_op jit(solution)/shard_map/reduce_scatter | solution.py:492
  218.5 1.7 copy-start.7
  253.9 53.5 %all-to-all-start.4 = ((bf16[32,16,2048]{2,1,0:T(8,128)(2,1)}), bf16[32,16,2048]{2,1,0:T(8,128)(2,1)}, u32[]{:S(2)}, u32[]{:S(2)}) async-start(bf16[32,16,2048]{2,1,0:T(8,128)(2,1)} %grad_rows.1), calls=%async_computation.5 | async-start | bytes 4194304 | tf_op jit(solution)/shard_map/all_to_all | solution.py:462
  277.7 1.3 copy-start.3
Sparse Core Ops, SparseCore 0:
  9.8 36.6 all-gather.3
  48.4 35.2 all-gather.5
  85.5 35.2 all-gather.7
  218.6 58.9 reduce-scatter.1

commit v3 on v2

--- a/solution.py
+++ b/solution.py
@@ -124,33 +124,32 @@
     )(received, shared)
 
 
-def route_kernel(capacity, ids_ref, gates_ref, cotangent_ref, put_ref, take_ref, mix_ref, send_ref):
+def slots_of(ids_ref, capacity):
     tokens = ids_ref.shape[1]
-    slots = put_ref.shape[0]
     ids = ids_ref[0]
-    gates = gates_ref[0].astype(F32)
     lane = lax.broadcasted_iota(jnp.int32, (tokens, tokens), 1)
     sub = lax.broadcasted_iota(jnp.int32, (tokens, tokens), 0)
     named = [(lane == ids[:, k : k + 1]).astype(F32) for k in range(2)]
     earlier = (lane < sub).astype(BF16)
     before = dot_nn(earlier, (named[0] + named[1]).astype(BF16))
-    slot = [
+    return [
         ids[:, k : k + 1].astype(F32) * capacity
         + jnp.sum(before * named[k], axis=1, keepdims=True)
         for k in range(2)
     ]
-    flat = [jnp.transpose(jnp.broadcast_to(slot[k], (tokens, tokens)))[0:1] for k in range(2)]
-    flat_gate = [
-        jnp.transpose(jnp.broadcast_to(gates[:, k : k + 1], (tokens, tokens)))[0:1]
-        for k in range(2)
-    ]
-    along = lax.broadcasted_iota(jnp.int32, (tokens, slots), 1).astype(F32)
+
+
+def across(column):
+    tokens = column.shape[0]
+    return jnp.transpose(jnp.broadcast_to(column, (tokens, tokens)))[0:1]
+
+
+def route_kernel(capacity, ids_ref, gates_ref, cotangent_ref, put_ref, send_ref):
+    slots, tokens = put_ref.shape
+    gates = gates_ref[0].astype(F32)
+    flat = [across(column) for column in slots_of(ids_ref, capacity)]
+    flat_gate = [across(gates[:, k : k + 1]) for k in range(2)]
     down = lax.broadcasted_iota(jnp.int32, (slots, tokens), 0).astype(F32)
-    hit = [along == slot[k] for k in range(2)]
-    take_ref[...] = jnp.where(hit[0] | hit[1], 1.0, 0.0).astype(BF16)
-    mix_ref[...] = jnp.where(
-        hit[0], gates[:, 0:1], jnp.where(hit[1], gates[:, 1:2], 0.0)
-    ).astype(BF16)
     fall = [down == flat[k] for k in range(2)]
     put_ref[...] = jnp.where(fall[0] | fall[1], 1.0, 0.0).astype(BF16)
     weigh = jnp.where(fall[0], flat_gate[0], jnp.where(fall[1], flat_gate[1], 0.0)).astype(BF16)
@@ -167,8 +166,6 @@
         functools.partial(route_kernel, capacity),
         out_shape=(
             jax.ShapeDtypeStruct((slots, tokens), BF16),
-            jax.ShapeDtypeStruct((tokens, slots), BF16),
-            jax.ShapeDtypeStruct((tokens, slots), BF16),
             jax.ShapeDtypeStruct((slots // capacity, capacity, wide + extra), BF16),
         ),
         grid=(1,),
@@ -179,14 +176,34 @@
         ],
         out_specs=(
             pl.BlockSpec((slots, tokens), lambda i: (0, 0)),
-            pl.BlockSpec((tokens, slots), lambda i: (0, 0)),
-            pl.BlockSpec((tokens, slots), lambda i: (0, 0)),
             pl.BlockSpec((slots // capacity, capacity, wide), lambda i: (0, 0, 0)),
         ),
         compiler_params=params(),
         cost_estimate=cost(2 * slots * tokens * wide, 2 * (slots + tokens) * wide),
         name="route",
     )(ids, gates, cotangent)
+
+
+def back_kernel(capacity, ids_ref, gates_ref, take_ref, mix_ref):
+    gates = gates_ref[0].astype(F32)
+    slot = slots_of(ids_ref, capacity)
+    along = lax.broadcasted_iota(jnp.int32, take_ref.shape, 1).astype(F32)
+    hit = [along == slot[k] for k in range(2)]
+    take_ref[...] = jnp.where(hit[0] | hit[1], 1.0, 0.0).astype(BF16)
+    mix_ref[...] = jnp.where(
+        hit[0], gates[:, 0:1], jnp.where(hit[1], gates[:, 1:2], 0.0)
+    ).astype(BF16)
+
+
+def back(ids, gates, capacity, slots):
+    shape = jax.ShapeDtypeStruct((ids.shape[1], slots), BF16)
+    return pl.pallas_call(
+        functools.partial(back_kernel, capacity),
+        out_shape=(shape, shape),
+        compiler_params=params(),
+        cost_estimate=cost(10**6, 10**6),
+        name="back",
+    )(ids, gates)
 
 
 def norm_kernel(quarters, lengths_ref, att_ref, resid_ref, gain_ref, put_ref, stream_ref, inverse_ref, send_ref):
@@ -241,57 +258,104 @@
     )(lengths, att, resid, gain, put)
 
 
-def expert_kernel(x_ref, gh_ref, gate_ref, up_ref, down_ref, out_ref, inner_ref, acc_ref):
-    step = pl.program_id(0)
+def expert_kernel(
+    x_ref,
+    gh_hbm,
+    gate_hbm,
+    up_hbm,
+    down_hbm,
+    rows_hbm,
+    inner_hbm,
+    gh_ref,
+    gate_ref,
+    up_ref,
+    down_ref,
+    rows_ref,
+    inner_ref,
+    in_sems,
+    out_sems,
+):
+    fetches = [
+        pltpu.make_async_copy(source, target, in_sems.at[k])
+        for k, (source, target) in enumerate(
+            (
+                (gate_hbm, gate_ref),
+                (up_hbm, up_ref),
+                (gh_hbm, gh_ref),
+                (down_hbm, down_ref),
+            )
+        )
+    ]
+    for fetch in fetches:
+        fetch.start()
+    stores = []
+
+    def store(source, target):
+        copy = pltpu.make_async_copy(source, target, out_sems.at[len(stores)])
+        copy.start()
+        stores.append(copy)
+
+    fetches[0].wait()
     x = flat_rows(x_ref)
     gate_pre = dot_nt(x, gate_ref[0])
+    fetches[1].wait()
     up_pre = dot_nt(x, up_ref[0])
     sigmoid = 1.0 / (1.0 + jnp.exp(-gate_pre))
     silu = gate_pre * sigmoid
-    hidden = (silu * up_pre).astype(BF16)
-    inner_ref[2] = hidden
-    product = dot_nn(hidden, down_ref[0])
-
-    @pl.when(step == 0)
-    def _():
-        acc_ref[...] = product
-
-    @pl.when((step > 0) & (step < pl.num_programs(0) - 1))
-    def _():
-        acc_ref[...] += product
-
-    @pl.when(step == pl.num_programs(0) - 1)
-    def _():
-        out_ref[...] = (acc_ref[...] + product).astype(BF16).reshape(out_ref.shape)
-
+    inner_ref[2] = (silu * up_pre).astype(BF16)
+    store(inner_ref.at[2], inner_hbm.at[2])
+    fetches[2].wait()
     grad_hidden = gh_ref[...]
     inner_ref[0] = (
         grad_hidden * up_pre * sigmoid * (1.0 + gate_pre * (1.0 - sigmoid))
     ).astype(BF16)
+    store(inner_ref.at[0], inner_hbm.at[0])
     inner_ref[1] = (grad_hidden * silu).astype(BF16)
+    store(inner_ref.at[1], inner_hbm.at[1])
+    fetches[3].wait()
+    owners, capacity, width = x_ref.shape
+    half = width // 2
+    for k in range(2):
+        lanes = slice(k * half, (k + 1) * half)
+        product = dot_nn(inner_ref[2], down_ref[0, :, lanes]).astype(BF16)
+        rows_ref[:, :, lanes] = product.reshape(owners, capacity, half)
+        store(rows_ref.at[:, :, lanes], rows_hbm.at[:, :, lanes])
+    for k in range(2):
+        lanes = slice(k * half, (k + 1) * half)
+        product = dot_nn(inner_ref[0], gate_ref[0, :, lanes])
+        product = (product + dot_nn(inner_ref[1], up_ref[0, :, lanes])).astype(BF16)
+        lanes = slice(width + k * half, width + (k + 1) * half)
+        rows_ref[:, :, lanes] = product.reshape(owners, capacity, half)
+        store(rows_ref.at[:, :, lanes], rows_hbm.at[:, :, lanes])
+    for copy in stores:
+        copy.wait()
 
 
 def expert(x, grad_hidden, gate, up, down):
     owners, capacity, width = x.shape
     rows = owners * capacity
     units = gate.shape[1]
-    block = 256
-    weight = pl.BlockSpec((1, block, width), lambda i: (0, i, 0))
-    column = pl.BlockSpec((rows, block), lambda i: (0, i))
-    whole = pl.BlockSpec((owners, capacity, width), lambda i: (0, 0, 0))
+    hbm = pl.BlockSpec(memory_space=pl.ANY)
+    out = (owners, capacity, 2 * width)
+    inner = (3, rows, units)
     return pl.pallas_call(
         expert_kernel,
-        grid=(units // block,),
-        in_specs=[whole, column, weight, weight, weight],
-        out_specs=(whole, pl.BlockSpec((3, rows, block), lambda i: (0, 0, i))),
-        out_shape=(
-            jax.ShapeDtypeStruct(x.shape, BF16),
-            jax.ShapeDtypeStruct((3, rows, units), BF16),
-        ),
-        scratch_shapes=[pltpu.VMEM((rows, width), F32)],
-        compiler_params=params(60),
+        in_specs=[pl.BlockSpec(memory_space=pltpu.VMEM)] + [hbm] * 4,
+        out_specs=(hbm, hbm),
+        out_shape=(pltpu.HBM(out, BF16), pltpu.HBM(inner, BF16)),
+        scratch_shapes=[
+            pltpu.VMEM(grad_hidden.shape, F32),
+            pltpu.VMEM(gate.shape, BF16),
+            pltpu.VMEM(up.shape, BF16),
+            pltpu.VMEM(down.shape, BF16),
+            pltpu.VMEM(out, BF16),
+            pltpu.VMEM(inner, BF16),
+            pltpu.SemaphoreType.DMA((4,)),
+            pltpu.SemaphoreType.DMA((7,)),
+        ],
+        compiler_params=params(44),
         cost_estimate=cost(
-            6 * rows * width * units, 4 * rows * width + 6 * units * width, rows * units
+            10 * rows * width * units, 6 * rows * width + 6 * units * width, rows * units
         ),
         name="expert",
     )(x, grad_hidden, gate, up, down)
@@ -319,63 +383,6 @@
         cost_estimate=cost(2 * rows * units * width, 2 * width * (rows + units) + 4 * rows * units),
         name="grad_hidden",
     )(shared, down)
-
-
-def rows_kernel(inner_ref, gate_ref, up_ref, out_ref, acc_ref):
-    step = pl.program_id(0)
-    product = dot_nn(inner_ref[0], gate_ref[0]) + dot_nn(inner_ref[1], up_ref[0])
-
-    @pl.when(step == 0)
-    def _():
-        acc_ref[...] = product
-
-    @pl.when((step > 0) & (step < pl.num_programs(0) - 1))
-    def _():
-        acc_ref[...] += product
-
-    @pl.when(step == pl.num_programs(0) - 1)
-    def _():
-        out_ref[...] = (acc_ref[...] + product).astype(BF16).reshape(out_ref.shape)
-
-
-def row_grads(inner, gate, up, capacity):
-    _, rows, units = inner.shape
-    width = gate.shape[2]
-    block = 256
-    weight = pl.BlockSpec((1, block, width), lambda i: (0, i, 0))
-    shape = (rows // capacity, capacity, width)
-    return pl.pallas_call(
-        rows_kernel,
-        grid=(units // block,),
-        in_specs=[pl.BlockSpec((2, rows, block), lambda i: (0, 0, i)), weight, weight],
-        out_specs=pl.BlockSpec(shape, lambda i: (0, 0, 0)),
-        out_shape=jax.ShapeDtypeStruct(shape, BF16),
-        scratch_shapes=[pltpu.VMEM((rows, width), F32)],
-        compiler_params=params(),
-        cost_estimate=cost(
-            4 * rows * units * width, 4 * units * width + 2 * rows * (width + 2 * units)
-        ),
-        name="grad_rows",
-    )(inner, gate, up)
-
-
-def mix_kernel(mix_ref, home_ref, out_ref):
-    for start in range(0, home_ref.shape[2], 512):
-        lanes = slice(start, start + 512)
-        home = home_ref[:, :, lanes].reshape(mix_ref.shape[1], 512)
-        out_ref[0, :, lanes] = dot_nn(mix_ref[...], home).astype(BF16)
-
-
-def mixed(mix, home):
-    tokens, slots = mix.shape
-    width = home.shape[2]
-    return pl.pallas_call(
-        mix_kernel,
-        out_shape=jax.ShapeDtypeStruct((1, tokens, width), BF16),
-        compiler_params=params(),
-        cost_estimate=cost(LONG, LONG // 1000),
-        name="mixture",
-    )(mix, home)
 
 
 def partial_kernel(inner_ref, x_ref, grad_out_ref, out_ref):
@@ -405,53 +412,67 @@
         in_specs=[pl.BlockSpec((1, rows, block), lambda k, i: (k, 0, i)), whole, whole],
         out_specs=pl.BlockSpec((block, width), lambda k, i: (k * count + i, 0)),
         out_shape=jax.ShapeDtypeStruct((kinds * units, width), BF16),
-        compiler_params=params(58),
+        compiler_params=params(36),
         cost_estimate=cost(2 * kinds * rows * units * width, 4 * (kinds * units + rows) * width),
         name="partials",
     )(inner, x, shared)
 
 
-def widen_kernel(in_ref, *out_refs):
-    units = out_refs[0].shape[1]
-    for k, out_ref in enumerate(out_refs):
-        out_ref[0] = in_ref[k * units : (k + 1) * units].astype(F32)
+def widen_kernel(*refs):
+    for in_ref, out_ref in zip(refs[:3], refs[3:]):
+        out_ref[0] = in_ref[...].astype(F32)
 
 
 def widen(grads, units):
     rows, width = grads.shape
+    block = 256
+    count = units // block
     return pl.pallas_call(
         widen_kernel,
-        out_shape=(jax.ShapeDtypeStruct((1, units, width), F32),) * (rows // units),
+        grid=(count,),
+        in_specs=[
+            pl.BlockSpec((block, width), lambda i, k=k: (k * count + i, 0)) for k in range(3)
+        ],
+        out_specs=(pl.BlockSpec((1, block, width), lambda i: (0, i, 0)),) * 3,
+        out_shape=(jax.ShapeDtypeStruct((1, units, width), F32),) * 3,
         compiler_params=params(),
         cost_estimate=cost(0, 6 * rows * width),
         name="widen",
-    )(grads)
-
-
-def finish_kernel(take_ref, home_ref, stream_ref, inverse_ref, gain_ref, out_ref):
+    )(grads, grads, grads)
+
+
+def finish_kernel(take_ref, mix_ref, home_ref, stream_ref, inverse_ref, gain_ref, mixture_ref, out_ref):
     width = stream_ref.shape[1]
+    slots = take_ref.shape[1]
+    wide = 512
     inverse = inverse_ref[:, 0:1]
     total = 0.0
-    for start in range(0, width, 512):
-        lanes = slice(start, start + 512)
-        home = home_ref[:, :, lanes].reshape(take_ref.shape[1], 512)
+    for start in range(0, width, wide):
+        lanes = slice(start, start + wide)
+        home = home_ref[:, :, width + start : width + start + wide].reshape(slots, wide)
         scaled = dot_nn(take_ref[...], home) * gain_ref[:, lanes]
         out_ref[0, :, lanes] = scaled
         total = total + jnp.sum(stream_ref[:, lanes] * scaled, axis=1, keepdims=True)
     factor = inverse * inverse * inverse * (total / width)
-    out_ref[0] = inverse * out_ref[0] - stream_ref[...] * factor
-
-
-def finish(take, home, stream, inverse, gain):
+    for start in range(0, width, wide):
+        lanes = slice(start, start + wide)
+        out_ref[0, :, lanes] = inverse * out_ref[0, :, lanes] - stream_ref[:, lanes] * factor
+        home = home_ref[:, :, lanes].reshape(slots, wide)
+        mixture_ref[0, :, lanes] = dot_nn(mix_ref[...], home).astype(BF16)
+
+
+def finish(take, mix, home, stream, inverse, gain):
     tokens, width = stream.shape
-    slots = take.shape[1]
     return pl.pallas_call(
         finish_kernel,
-        out_shape=jax.ShapeDtypeStruct((1, tokens, width), F32),
-        compiler_params=params(),
-        cost_estimate=cost(2 * slots * tokens * width, 2 * (slots + 4 * tokens) * width),
+        out_shape=(
+            jax.ShapeDtypeStruct((1, tokens, width), BF16),
+            jax.ShapeDtypeStruct((1, tokens, width), F32),
+        ),
+        compiler_params=params(),
+        cost_estimate=cost(LONG, LONG // 1000),
         name="finish",
-    )(take, home, stream, inverse, gain)
+    )(take, mix, home, stream, inverse, gain)
 
 
 def in_hbm(values):
@@ -477,29 +498,24 @@
     up_full = lax.all_gather(w_up, "dp", axis=2, tiled=True)
 
     received = swap(pack(lengths, qkv, quarters))
-    put, take, mix, adjoint_send = route(
+    put, adjoint_send = route(
         expert_ids, gate_vals, cotangent, capacity, slots, width // quarters
     )
+    take, mix = back(expert_ids, gate_vals, capacity, slots)
     shared = swap(in_hbm(attend(received, in_hbm(adjoint_send), head_size)))
     stream, inverse, normed_send = norm(lengths, shared, resid, gain, put, quarters)
     x_rows = swap(in_hbm(normed_send))
 
     gate_full, up_full, down_full = in_hbm(gate_full), in_hbm(up_full), in_hbm(down_full)
     grad_hidden = in_hbm(hidden_grad(shared, down_full))
-    expert_out, inner = expert(x_rows, grad_hidden, gate_full, up_full, down_full)
-    out_home = swap(in_hbm(expert_out))
+    rows, inner = expert(x_rows, grad_hidden, gate_full, up_full, down_full)
+    home = swap(rows)
 
     grads = lax.psum_scatter(
         partials(inner, x_rows, shared), "dp", scatter_dimension=1, tiled=True
     )
-    grad_gate, grad_up, grad_down = widen(grads, w_gate.shape[1])
-    grad_rows = in_hbm(row_grads(inner, gate_full, up_full, capacity))
-    grad_rows, out_home = lax.optimization_barrier((grad_rows, out_home))
-    grad_home = swap(grad_rows)
-
-    mixture = mixed(mix, out_home)
-    take, grad_gate = lax.optimization_barrier((take, grad_gate))
-    grad_stream = finish(take, grad_home, stream, inverse, gain)
+    grad_gate, grad_up, grad_down = widen(in_hbm(grads), w_gate.shape[1])
+    mixture, grad_stream = finish(take, mix, home, stream, inverse, gain)
     return (mixture, grad_stream, grad_gate, grad_up, grad_down)
 
 

time: 318 us -> 319 us (level)
  waiting for transfers between devices: 207 us -> 217 us
  Pallas kernels: 52.6 us -> 45.6 us
  starting transfers between devices: 36.2 us -> 30.4 us
  local copies, waits for them, and re-layouts: 7.21 us -> 10.9 us
    all_to_all x5 -> x4, waiting for transfers between devices: 190 us -> 214 us  [swap(): return lax.all_to_all(values, axis, split_axis=0, concat_axis=0, tiled=True)]
    reduce_scatter x1, waiting for transfers between devices: 14.8 us -> 0.01 us  [body(): lax.psum_scatter(partials(inner, x_rows, shared), 'dp', scatter_dimension...]
    all_to_all x5 -> x4, starting transfers between devices: 35.8 us -> 30.2 us  [swap(): return lax.all_to_all(values, axis, split_axis=0, concat_axis=0, tiled=True)]
    pallas_call x5 -> x4, Pallas kernels: 27.3 us -> 22.9 us  [the longest x1 14.8 us: expert(): pl.pallas_call(expert_kernel, in_specs=[pl.BlockSpec(memory_space=pltpu.V...]
    unnamed x22 -> x24, local copies, waits for them, and re-layouts: 7.21 us -> 10.9 us
  transfers between devices with their start and end apart: 9 -> 8, of which waited for: 6 -> 4; matrix products, arithmetic and copies ran while one was open for 0% -> 0% of each run, Pallas kernels for 12% -> 9%
where the time goes in v3:
time: 319 us; the launch traced here: 318 us
  waiting for transfers between devices  217 us (68%)
  Pallas kernels  45.6 us (14%)
  starting transfers between devices  30.4 us (10%)
  between operations  14.5 us (5%)
  local copies, waits for them, and re-layouts  10.9 us (3%)
    all_to_all x4, waiting for transfers between devices, swap(): return lax.all_to_all(values, axis, split_axis=0, concat_axis=0, tiled=True)  214 us
    all_to_all x4, starting transfers between devices, swap(): return lax.all_to_all(values, axis, split_axis=0, concat_axis=0, tiled=True)  30.2 us
    pallas_call x1, Pallas kernels, expert(): pl.pallas_call(expert_kernel, in_specs=[pl.BlockSpec(memory_space=pltpu.V...  14.8 us
    unnamed x24, local copies, waits for them, and re-layouts  10.9 us
    pallas_call x1, Pallas kernels, partials(): pl.pallas_call(partial_kernel, grid=(kinds, count), in_specs=[pl.BlockSpe...  9.19 us
  transfers between devices with their start and end apart: 8, of which 4 were waited for; matrix products, arithmetic and copies ran while one was open for 0% of the time, Pallas kernels for 9%

profile of v3, /device:TPU:16, one launch (start us, length us, event | category | flops | bytes accessed | tf_op | source)
XLA Modules:
  0.0 317.9 jit_solution(14125271131604607217)
XLA Ops:
  7.2 0.7 all-gather.4.cloned.1.call-update
  8.6 1.4 copy-done.3
  10.0 1.7 pack_qkv.1
  11.7 11.3 %all-to-all-start = ((bf16[32,3,16,512]{3,2,1,0:T(8,128)(2,1)}), bf16[32,3,16,512]{3,2,1,0:T(8,128)(2,1)S(1)}, u32[]{:S(2)}, u32[]{:S(2)}) async-start(bf16[32,3,16,512]{3,2,1,0:T(8,128)(2,1)} %pack_qkv.1), calls=%async_computation | async-start | bytes 3145728 | tf_op jit(solution)/shard_map/all_to_all | solution.py:483
  23.0 0.0 all-gather.6.cloned.1.call-start
  23.1 0.7 all-gather.6.cloned.1.call-update
  23.8 0.1 copy.16.ids_ref
  23.9 0.1 copy.17.gates_ref
  24.0 1.2 route.1
  25.3 1.5 copy-done
  26.7 35.4 %all-to-all-done.in_ref = bf16[32,3,16,512]{3,2,1,0:T(8,128)(2,1)S(1)} async-done(((bf16[32,3,16,512]{3,2,1,0:T(8,128)(2,1)}), bf16[32,3,16,512]{3,2,1,0:T(8,128)(2,1)S(1)}, u32[]{:S(2)}, u32[]{:S(2)}) %all-to-all-start) | async-done | bytes 1572896 | tf_op jit(solution)/shard_map/all_to_all | solution.py:483
  62.1 2.5 attend.1
  64.6 6.0 %all-to-all-start.1 = ((bf16[32,16,2560]{2,1,0:T(8,128)(2,1)}), bf16[32,16,2560]{2,1,0:T(8,128)(2,1)}, u32[]{:S(2)}, u32[]{:S(2)}) async-start(bf16[32,16,2560]{2,1,0:T(8,128)(2,1)} %attend.1), calls=%async_computation.1 | async-start | bytes 5242880 | tf_op jit(solution)/shard_map/all_to_all | solution.py:483
  70.6 0.0 all-gather.8.cloned.1.call-start
  70.7 0.7 all-gather.8.cloned.1.call-update
  71.4 59.3 %all-to-all-done.1.att_ref.grad_out_ref = bf16[32,16,2560]{2,1,0:T(8,128)(2,1)} async-done(((bf16[32,16,2560]{2,1,0:T(8,128)(2,1)}), bf16[32,16,2560]{2,1,0:T(8,128)(2,1)}, u32[]{:S(2)}, u32[]{:S(2)}) %all-to-all-start.1) | async-done | bytes 2621472 | tf_op jit(solution)/shard_map/all_to_all | solution.py:483
  130.6 3.4 %norm.1 = (f32[128,2048]{1,0:T(8,128)S(1)}, f32[128,128]{1,0:T(8,128)S(1)}, bf16[32,16,2048]{2,1,0:T(8,128)(2,1)}) custom-call(s32[1]{0:T(128)S(6)} %copy.21.lengths_ref, bf16[32,16,2560]{2,1,0:T(8,128)(2,1)} %all-to-all-done.1.att_ref.grad_out_ref, bf16[1,128,2048]{2,1,0:T(8,128)(2,1)S(1)} %copy-done.4, f32[1,2048]{1,0:T(1,128)S(1)} %bitcast.1, ...), custom_call_target="tpu_custom_call" | custom-call | flops 268435456 | bytes 4194304 | tf_op jit(solution)/shard_map/norm/pallas_call | solution.py:235
  134.0 6.3 %all-to-all-start.2 = ((bf16[32,16,2048]{2,1,0:T(8,128)(2,1)}), bf16[32,16,2048]{2,1,0:T(8,128)(2,1)S(1)}, u32[]{:S(2)}, u32[]{:S(2)}) async-start(bf16[32,16,2048]{2,1,0:T(8,128)(2,1)} %get-tuple-element.23), calls=%async_computation.2 | async-start | bytes 4194304 | tf_op jit(solution)/shard_map/all_to_all | solution.py:483
  140.3 4.7 %grad_hidden.1.gh_hbm = f32[512,768]{1,0:T(8,128)S(1)} custom-call(bf16[32,16,2560]{2,1,0:T(8,128)(2,1)} %all-to-all-done.1.att_ref.grad_out_ref, bf16[1,768,2048]{2,1,0:T(8,128)(2,1)} %all-gather.4.cloned.1.call-done.down_ref.down_hbm), custom_call_target="tpu_custom_call" | custom-call | flops 1610612736 | bytes 6815744 | tf_op jit(solution)/shard_map/grad_hidden/pallas_call | solution.py:373
  145.1 1.2 copy-done.2
  146.2 41.5 %all-to-all-done.2.x_ref = bf16[32,16,2048]{2,1,0:T(8,128)(2,1)S(1)} async-done(((bf16[32,16,2048]{2,1,0:T(8,128)(2,1)}), bf16[32,16,2048]{2,1,0:T(8,128)(2,1)S(1)}, u32[]{:S(2)}, u32[]{:S(2)}) %all-to-all-start.2) | async-done | bytes 2097184 | tf_op jit(solution)/shard_map/all_to_all | solution.py:483
  187.7 1.3 copy-done.8
  189.1 14.8 %expert.1 = (bf16[32,16,4096]{2,1,0:T(8,128)(2,1)}, bf16[3,512,768]{2,1,0:T(8,128)(2,1)}) custom-call(bf16[32,16,2048]{2,1,0:T(8,128)(2,1)} %copy-done.8, f32[512,768]{1,0:T(8,128)} %copy-done.2, bf16[1,768,2048]{2,1,0:T(8,128)(2,1)} %all-gather.6.cloned.1.call-done.gate_hbm, bf16[1,768,2048]{2,1,0:T(8,128)(2,1)} %all-gather.8.cloned.1.call-done.up_hbm, ...), custom_call_target="tpu_custom_call" | custom-call | flops 8053063680 | bytes 15728640 | tf_op jit(solution)/shard_map/expert/pallas_call | solution.py:341
  203.9 6.6 %all-to-all-start.3 = ((bf16[32,16,4096]{2,1,0:T(8,128)(2,1)}), bf16[32,16,4096]{2,1,0:T(8,128)(2,1)}, u32[]{:S(2)}, u32[]{:S(2)}) async-start(bf16[32,16,4096]{2,1,0:T(8,128)(2,1)} %get-tuple-element.24), calls=%async_computation.3 | async-start | bytes 8388608 | tf_op jit(solution)/shard_map/all_to_all | solution.py:483
  210.5 0.0 reduce-scatter.2.cloned.1.call-start
  210.6 0.4 back.1
  211.0 1.7 copy-done.7
  212.7 9.2 %partials.1 = bf16[2304,2048]{1,0:T(8,128)(2,1)S(1)} custom-call(bf16[3,512,768]{2,1,0:T(8,128)(2,1)S(1)} %copy-done.7, bf16[32,16,2048]{2,1,0:T(8,128)(2,1)} %copy-done.8, bf16[32,16,2560]{2,1,0:T(8,128)(2,1)} %all-to-all-done.1.att_ref.grad_out_ref), custom_call_target="tpu_custom_call" | custom-call | flops 4831838208 | bytes 23068672 | tf_op jit(solution)/shard_map/partials/pallas_call | solution.py:409
  221.9 3.6 %copy-done.1 = bf16[2304,2048]{1,0:T(8,128)(2,1)} copy-done((bf16[2304,2048]{1,0:T(8,128)(2,1)}, bf16[2304,2048]{1,0:T(8,128)(2,1)S(1)}, u32[]{:S(2)}) %copy-start.1) | copy-done | bytes 9437208
  225.5 78.2 %all-to-all-done.3.home_ref = bf16[32,16,4096]{2,1,0:T(8,128)(2,1)} async-done(((bf16[32,16,4096]{2,1,0:T(8,128)(2,1)}), bf16[32,16,4096]{2,1,0:T(8,128)(2,1)}, u32[]{:S(2)}, u32[]{:S(2)}) %all-to-all-start.3) | async-done | bytes 4194336 | tf_op jit(solution)/shard_map/all_to_all | solution.py:483
  303.7 4.2 %finish.1 = (bf16[1,128,2048]{2,1,0:T(8,128)(2,1)}, f32[1,128,2048]{2,1,0:T(8,128)}) custom-call(bf16[128,512]{1,0:T(8,128)(2,1)S(1)} %get-tuple-element.19.take_ref, bf16[128,512]{1,0:T(8,128)(2,1)S(1)} %get-tuple-element.20.mix_ref, bf16[32,16,4096]{2,1,0:T(8,128)(2,1)} %all-to-all-done.3.home_ref, f32[128,2048]{1,0:T(8,128)S(1)} %get-tuple-element.25.stream_ref, ...), custom_call_target="tpu_custom_call" | custom-call | flops 999999986991104 | bytes 999999995904 | tf_op jit(solution)/shard_map/finish/pallas_call | solution.py:466
  307.8 3.5 %widen.1 = (f32[1,768,256]{2,1,0:T(8,128)}, f32[1,768,256]{2,1,0:T(8,128)}, f32[1,768,256]{2,1,0:T(8,128)}) custom-call(bf16[2304,256]{1,0:T(8,128)(2,1)} %reduce-scatter.2.cloned.1.call-done.refs_0_.refs_1_.refs_2_, bf16[2304,256]{1,0:T(8,128)(2,1)} %reduce-scatter.2.cloned.1.call-done.refs_0_.refs_1_.refs_2_, ...), custom_call_target="tpu_custom_call" | custom-call | bytes 3538944 | tf_op jit(solution)/shard_map/widen/pallas_call | solution.py:430
  (22 shorter events, 0.1 us)
Async XLA Ops:
  7.2 133.2 %all-gather.4.cloned.1.call-start = ((), (), s32[]{:S(2)}) async-start(), calls=%async_computation.5 | async-start | bytes 3538944 | tf_op jit(solution)/shard_map/all_gather | solution.py:496
  8.5 1.4 copy-start.3
  10.0 13.8 %copy-start.9 = (s32[1,128,2]{1,2,0:T(2,128)S(1)}, s32[1,128,2]{1,2,0:T(2,128)}, u32[]{:S(2)}) copy-start(s32[1,128,2]{1,2,0:T(2,128)} %param.14) | copy-start | bytes 3076
  10.0 13.9 %copy-start.10 = (bf16[1,128,2]{1,2,0:T(2,128)(2,1)S(1)}, bf16[1,128,2]{1,2,0:T(2,128)(2,1)}, u32[]{:S(2)}) copy-start(bf16[1,128,2]{1,2,0:T(2,128)(2,1)} %param.15) | copy-start | bytes 1540
  10.0 14.1 %copy-start.6 = (bf16[1,128,2048]{2,1,0:T(8,128)(2,1)S(1)}, bf16[1,128,2048]{2,1,0:T(8,128)(2,1)}, u32[]{:S(2)}) copy-start(bf16[1,128,2048]{2,1,0:T(8,128)(2,1)} %cotangent_ref.1) | copy-start | bytes 1572868
  11.7 50.4 %all-to-all-start = ((bf16[32,3,16,512]{3,2,1,0:T(8,128)(2,1)}), bf16[32,3,16,512]{3,2,1,0:T(8,128)(2,1)S(1)}, u32[]{:S(2)}, u32[]{:S(2)}) async-start(bf16[32,3,16,512]{3,2,1,0:T(8,128)(2,1)} %pack_qkv.1), calls=%async_computation | async-start | bytes 3145728 | tf_op jit(solution)/shard_map/all_to_all | solution.py:483
  23.0 123.2 %all-gather.6.cloned.1.call-start = ((), (), s32[]{:S(2)}) async-start(), calls=%async_computation.6 | async-start | bytes 3538944 | tf_op jit(solution)/shard_map/all_gather | solution.py:497
  25.2 1.5 copy-start
  64.6 66.0 %copy-start.4 = (bf16[1,128,2048]{2,1,0:T(8,128)(2,1)S(1)}, bf16[1,128,2048]{2,1,0:T(8,128)(2,1)}, u32[]{:S(2)}) copy-start(bf16[1,128,2048]{2,1,0:T(8,128)(2,1)} %resid_ref.1) | copy-start | bytes 1572868
  64.6 66.0 %copy-start.5 = (f32[2048]{0:T(1024)S(1)}, f32[2048]{0:T(1024)}, u32[]{:S(2)}) copy-start(f32[2048]{0:T(1024)} %param.13) | copy-start | bytes 24580
  64.6 66.0 %all-to-all-start.1 = ((bf16[32,16,2560]{2,1,0:T(8,128)(2,1)}), bf16[32,16,2560]{2,1,0:T(8,128)(2,1)}, u32[]{:S(2)}, u32[]{:S(2)}) async-start(bf16[32,16,2560]{2,1,0:T(8,128)(2,1)} %attend.1), calls=%async_computation.1 | async-start | bytes 5242880 | tf_op jit(solution)/shard_map/all_to_all | solution.py:483
  70.6 75.6 %all-gather.8.cloned.1.call-start = ((), (), s32[]{:S(2)}) async-start(), calls=%async_computation.7 | async-start | bytes 3538944 | tf_op jit(solution)/shard_map/all_gather | solution.py:498
  134.0 53.7 %all-to-all-start.2 = ((bf16[32,16,2048]{2,1,0:T(8,128)(2,1)}), bf16[32,16,2048]{2,1,0:T(8,128)(2,1)S(1)}, u32[]{:S(2)}, u32[]{:S(2)}) async-start(bf16[32,16,2048]{2,1,0:T(8,128)(2,1)} %get-tuple-element.23), calls=%async_computation.2 | async-start | bytes 4194304 | tf_op jit(solution)/shard_map/all_to_all | solution.py:483
  145.1 1.2 copy-start.2
  187.7 1.3 copy-start.8
  203.9 99.8 %all-to-all-start.3 = ((bf16[32,16,4096]{2,1,0:T(8,128)(2,1)}), bf16[32,16,4096]{2,1,0:T(8,128)(2,1)}, u32[]{:S(2)}, u32[]{:S(2)}) async-start(bf16[32,16,4096]{2,1,0:T(8,128)(2,1)} %get-tuple-element.24), calls=%async_computation.3 | async-start | bytes 8388608 | tf_op jit(solution)/shard_map/all_to_all | solution.py:483
  210.5 97.3 %reduce-scatter.2.cloned.1.call-start = ((), (), s32[]{:S(2)}) async-start(), calls=%async_computation.8 | async-start | bytes 10616832 | tf_op jit(solution)/shard_map/reduce_scatter | solution.py:514
  211.0 1.7 copy-start.7
  221.9 3.6 %copy-start.1 = (bf16[2304,2048]{1,0:T(8,128)(2,1)}, bf16[2304,2048]{1,0:T(8,128)(2,1)S(1)}, u32[]{:S(2)}) copy-start(bf16[2304,2048]{1,0:T(8,128)(2,1)S(1)} %partials.1) | copy-start | bytes 28311556
Sparse Core Ops, SparseCore 0:
  9.8 36.6 all-gather.3
  48.4 35.2 all-gather.5
  85.5 35.2 all-gather.7
  225.6 58.9 reduce-scatter.1

commit v4 on v3

--- a/solution.py
+++ b/solution.py
@@ -206,7 +206,19 @@
     )(ids, gates)
 
 
-def norm_kernel(quarters, lengths_ref, att_ref, resid_ref, gain_ref, put_ref, stream_ref, inverse_ref, send_ref):
+def norm_kernel(
+    quarters,
+    lengths_ref,
+    att_ref,
+    resid_ref,
+    gain_ref,
+    put_ref,
+    stream_ref,
+    inverse_ref,
+    send_hbm,
+    send_ref,
+    sems,
+):
     blocks, times, wide = att_ref.shape
     for block in range(blocks):
         at, quarter = block // quarters, block % quarters
@@ -220,11 +232,20 @@
     stream = stream_ref[...]
     inverse = 1.0 / jnp.sqrt(jnp.sum(stream * stream, axis=1, keepdims=True) / width + 1e-05)
     inverse_ref[...] = jnp.broadcast_to(inverse, inverse_ref.shape)
+    stores = []
     for start in range(0, width, 512):
         lanes = slice(start, start + 512)
         normed = (stream_ref[:, lanes] * inverse * gain_ref[:, lanes]).astype(BF16)
         rows = dot_nn(put_ref[...], normed).astype(BF16)
         send_ref[:, :, lanes] = rows.reshape(send_ref.shape[0], send_ref.shape[1], 512)
+        stores.append(
+            pltpu.make_async_copy(
+                send_ref.at[:, :, lanes], send_hbm.at[:, :, lanes], sems.at[len(stores)]
+            )
+        )
+        stores[-1].start()
+    for copy in stores:
+        copy.wait()
 
 
 def norm(lengths, att, resid, gain, put, quarters):
@@ -245,13 +266,17 @@
         out_specs=(
             pl.BlockSpec((tokens, width), lambda i: (0, 0)),
             pl.BlockSpec((tokens, 128), lambda i: (0, 0)),
-            pl.BlockSpec((blocks, slots // blocks, width), lambda i: (0, 0, 0)),
+            pl.BlockSpec(memory_space=pl.ANY),
         ),
         out_shape=(
             jax.ShapeDtypeStruct((tokens, width), F32),
             jax.ShapeDtypeStruct((tokens, 128), F32),
-            jax.ShapeDtypeStruct((blocks, slots // blocks, width), BF16),
+            pltpu.HBM((blocks, slots // blocks, width), BF16),
         ),
+        scratch_shapes=[
+            pltpu.VMEM((blocks, slots // blocks, width), BF16),
+            pltpu.SemaphoreType.DMA((width // 512,)),
+        ],
         compiler_params=params(),
         cost_estimate=cost(2 * slots * tokens * width, 2 * (slots + 4 * tokens) * width),
         name="norm",
@@ -340,7 +365,8 @@
     inner = (3, rows, units)
     return pl.pallas_call(
         expert_kernel,
-        in_specs=[pl.BlockSpec(memory_space=pltpu.VMEM)] + [hbm] * 4,
+        grid=(1,),
+        in_specs=[pl.BlockSpec(x.shape, lambda i: (0, 0, 0))] + [hbm] * 4,
         out_specs=(hbm, hbm),
         out_shape=(pltpu.HBM(out, BF16), pltpu.HBM(inner, BF16)),
         scratch_shapes=[
@@ -353,7 +379,7 @@
             pltpu.SemaphoreType.DMA((4,)),
             pltpu.SemaphoreType.DMA((7,)),
         ],
-        compiler_params=params(44),
+        compiler_params=params(60),
         cost_estimate=cost(
             10 * rows * width * units, 6 * rows * width + 6 * units * width, rows * units
         ),
@@ -412,63 +438,114 @@
         in_specs=[pl.BlockSpec((1, rows, block), lambda k, i: (k, 0, i)), whole, whole],
         out_specs=pl.BlockSpec((block, width), lambda k, i: (k * count + i, 0)),
         out_shape=jax.ShapeDtypeStruct((kinds * units, width), BF16),
-        compiler_params=params(36),
+        compiler_params=params(58),
         cost_estimate=cost(2 * kinds * rows * units * width, 4 * (kinds * units + rows) * width),
         name="partials",
     )(inner, x, shared)
 
 
-def widen_kernel(*refs):
-    for in_ref, out_ref in zip(refs[:3], refs[3:]):
-        out_ref[0] = in_ref[...].astype(F32)
+def widen_kernel(in_ref, *out_refs):
+    units = out_refs[0].shape[1]
+    for k, out_ref in enumerate(out_refs):
+        out_ref[0] = in_ref[k * units : (k + 1) * units].astype(F32)
 
 
 def widen(grads, units):
     rows, width = grads.shape
-    block = 256
-    count = units // block
     return pl.pallas_call(
         widen_kernel,
-        grid=(count,),
-        in_specs=[
-            pl.BlockSpec((block, width), lambda i, k=k: (k * count + i, 0)) for k in range(3)
-        ],
-        out_specs=(pl.BlockSpec((1, block, width), lambda i: (0, i, 0)),) * 3,
-        out_shape=(jax.ShapeDtypeStruct((1, units, width), F32),) * 3,
+        out_shape=(jax.ShapeDtypeStruct((1, units, width), F32),) * (rows // units),
         compiler_params=params(),
         cost_estimate=cost(0, 6 * rows * width),
         name="widen",
-    )(grads, grads, grads)
-
-
-def finish_kernel(take_ref, mix_ref, home_ref, stream_ref, inverse_ref, gain_ref, mixture_ref, out_ref):
+    )(grads)
+
+
+def finish_kernel(
+    take_ref,
+    mix_ref,
+    home_hbm,
+    stream_ref,
+    inverse_ref,
+    gain_ref,
+    mixture_hbm,
+    out_hbm,
+    home_ref,
+    mixture_ref,
+    out_ref,
+    in_sems,
+    out_sems,
+):
     width = stream_ref.shape[1]
     slots = take_ref.shape[1]
-    wide = 512
+    blocks = in_sems.shape[0]
+    wide = home_ref.shape[2] // blocks
+    half = blocks // 2
+    order = list(range(half, blocks)) + list(range(half))
+
+    def block(k):
+        return slice(k * wide, (k + 1) * wide)
+
+    fetches = {
+        k: pltpu.make_async_copy(
+            home_hbm.at[:, :, block(k)], home_ref.at[:, :, block(k)], in_sems.at[k]
+        )
+        for k in order
+    }
+    for k in order:
+        fetches[k].start()
+    total = 0.0
+    for k in range(half):
+        fetches[half + k].wait()
+        home = home_ref[:, :, block(half + k)].reshape(slots, wide)
+        scaled = dot_nn(take_ref[...], home) * gain_ref[:, block(k)]
+        out_ref[0, :, block(k)] = scaled
+        total = total + jnp.sum(stream_ref[:, block(k)] * scaled, axis=1, keepdims=True)
     inverse = inverse_ref[:, 0:1]
-    total = 0.0
-    for start in range(0, width, wide):
-        lanes = slice(start, start + wide)
-        home = home_ref[:, :, width + start : width + start + wide].reshape(slots, wide)
-        scaled = dot_nn(take_ref[...], home) * gain_ref[:, lanes]
-        out_ref[0, :, lanes] = scaled
-        total = total + jnp.sum(stream_ref[:, lanes] * scaled, axis=1, keepdims=True)
     factor = inverse * inverse * inverse * (total / width)
-    for start in range(0, width, wide):
-        lanes = slice(start, start + wide)
-        out_ref[0, :, lanes] = inverse * out_ref[0, :, lanes] - stream_ref[:, lanes] * factor
-        home = home_ref[:, :, lanes].reshape(slots, wide)
-        mixture_ref[0, :, lanes] = dot_nn(mix_ref[...], home).astype(BF16)
+    stores = []
+    for k in range(half):
+        out_ref[0, :, block(k)] = inverse * out_ref[0, :, block(k)] - stream_ref[:, block(k)] * factor
+        stores.append(
+            pltpu.make_async_copy(
+                out_ref.at[:, :, block(k)], out_hbm.at[:, :, block(k)], out_sems.at[k]
+            )
+        )
+        stores[-1].start()
+    for k in range(half):
+        fetches[k].wait()
+        home = home_ref[:, :, block(k)].reshape(slots, wide)
+        mixture_ref[0, :, block(k)] = dot_nn(mix_ref[...], home).astype(BF16)
+        stores.append(
+            pltpu.make_async_copy(
+                mixture_ref.at[:, :, block(k)], mixture_hbm.at[:, :, block(k)], out_sems.at[half + k]
+            )
+        )
+        stores[-1].start()
+    for copy in stores:
+        copy.wait()
 
 
 def finish(take, mix, home, stream, inverse, gain):
     tokens, width = stream.shape
+    vmem = pl.BlockSpec(memory_space=pltpu.VMEM)
+    hbm = pl.BlockSpec(memory_space=pl.ANY)
+    blocks = 8
     return pl.pallas_call(
         finish_kernel,
+        in_specs=[vmem, vmem, hbm, vmem, vmem, vmem],
+        out_specs=(hbm, hbm),
         out_shape=(
             jax.ShapeDtypeStruct((1, tokens, width), BF16),
             jax.ShapeDtypeStruct((1, tokens, width), F32),
         ),
+        scratch_shapes=[
+            pltpu.VMEM(home.shape, BF16),
+            pltpu.VMEM((1, tokens, width), BF16),
+            pltpu.VMEM((1, tokens, width), F32),
+            pltpu.SemaphoreType.DMA((blocks,)),
+            pltpu.SemaphoreType.DMA((blocks,)),
+        ],
         compiler_params=params(),
         cost_estimate=cost(LONG, LONG // 1000),
         name="finish",
@@ -504,7 +581,7 @@
     take, mix = back(expert_ids, gate_vals, capacity, slots)
     shared = swap(in_hbm(attend(received, in_hbm(adjoint_send), head_size)))
     stream, inverse, normed_send = norm(lengths, shared, resid, gain, put, quarters)
-    x_rows = swap(in_hbm(normed_send))
+    x_rows = swap(normed_send)
 
     gate_full, up_full, down_full = in_hbm(gate_full), in_hbm(up_full), in_hbm(down_full)
     grad_hidden = in_hbm(hidden_grad(shared, down_full))

time: 319 us -> 318 us (level)
  local copies, waits for them, and re-layouts: 10.9 us -> 5.63 us
    unnamed x24 -> x20, local copies, waits for them, and re-layouts: 10.9 us -> 5.63 us
where the time goes in v4:
time: 318 us; the launch traced here: 317 us
  waiting for transfers between devices  219 us (69%)
  Pallas kernels  47.2 us (15%)
  starting transfers between devices  30.4 us (10%)
  between operations  14.5 us (5%)
  local copies, waits for them, and re-layouts  5.63 us (2%)
    all_to_all x4, waiting for transfers between devices, swap(): return lax.all_to_all(values, axis, split_axis=0, concat_axis=0, tiled=True)  217 us
    all_to_all x4, starting transfers between devices, swap(): return lax.all_to_all(values, axis, split_axis=0, concat_axis=0, tiled=True)  30.2 us
    pallas_call x1, Pallas kernels, expert(): pl.pallas_call(expert_kernel, grid=(1,), in_specs=[pl.BlockSpec(x.shape,...  14.9 us
    pallas_call x1, Pallas kernels, partials(): pl.pallas_call(partial_kernel, grid=(kinds, count), in_specs=[pl.BlockSpe...  11.9 us
  transfers between devices with their start and end apart: 8, of which 4 were waited for; matrix products, arithmetic and copies ran while one was open for 0% of the time, Pallas kernels for 9%

profile of v4, /device:TPU:16, one launch (start us, length us, event | category | flops | bytes accessed | tf_op | source)
XLA Modules:
  0.0 316.9 jit_solution(5182115195307802114)
XLA Ops:
  7.2 0.0 all-gather.4.cloned.1.call-start
  7.2 0.7 all-gather.4.cloned.1.call-update
  8.6 1.4 copy-done.2
  10.0 1.7 pack_qkv.1
  11.7 11.3 %all-to-all-start = ((bf16[32,3,16,512]{3,2,1,0:T(8,128)(2,1)}), bf16[32,3,16,512]{3,2,1,0:T(8,128)(2,1)S(1)}, u32[]{:S(2)}, u32[]{:S(2)}) async-start(bf16[32,3,16,512]{3,2,1,0:T(8,128)(2,1)} %pack_qkv.1), calls=%async_computation | async-start | bytes 3145728 | tf_op jit(solution)/shard_map/all_to_all | solution.py:560
  23.0 0.0 all-gather.6.cloned.1.call-start
  23.1 0.7 all-gather.6.cloned.1.call-update
  23.8 0.1 copy.16.ids_ref
  23.9 0.1 copy.17.gates_ref
  24.0 1.2 route.1
  25.3 1.5 copy-done
  26.7 35.4 %all-to-all-done.in_ref = bf16[32,3,16,512]{3,2,1,0:T(8,128)(2,1)S(1)} async-done(((bf16[32,3,16,512]{3,2,1,0:T(8,128)(2,1)}), bf16[32,3,16,512]{3,2,1,0:T(8,128)(2,1)S(1)}, u32[]{:S(2)}, u32[]{:S(2)}) %all-to-all-start) | async-done | bytes 1572896 | tf_op jit(solution)/shard_map/all_to_all | solution.py:560
  62.1 2.5 attend.1
  64.6 6.0 %all-to-all-start.1 = ((bf16[32,16,2560]{2,1,0:T(8,128)(2,1)}), bf16[32,16,2560]{2,1,0:T(8,128)(2,1)}, u32[]{:S(2)}, u32[]{:S(2)}) async-start(bf16[32,16,2560]{2,1,0:T(8,128)(2,1)} %attend.1), calls=%async_computation.1 | async-start | bytes 5242880 | tf_op jit(solution)/shard_map/all_to_all | solution.py:560
  70.6 0.0 all-gather.8.cloned.1.call-start
  70.7 0.7 all-gather.8.cloned.1.call-update
  71.4 59.3 %all-to-all-done.1.att_ref.grad_out_ref = bf16[32,16,2560]{2,1,0:T(8,128)(2,1)} async-done(((bf16[32,16,2560]{2,1,0:T(8,128)(2,1)}), bf16[32,16,2560]{2,1,0:T(8,128)(2,1)}, u32[]{:S(2)}, u32[]{:S(2)}) %all-to-all-start.1) | async-done | bytes 2621472 | tf_op jit(solution)/shard_map/all_to_all | solution.py:560
  130.6 3.0 norm.1
  133.6 6.3 %all-to-all-start.2 = ((bf16[32,16,2048]{2,1,0:T(8,128)(2,1)}), bf16[32,16,2048]{2,1,0:T(8,128)(2,1)S(1)}, u32[]{:S(2)}, u32[]{:S(2)}) async-start(bf16[32,16,2048]{2,1,0:T(8,128)(2,1)} %get-tuple-element.23), calls=%async_computation.2 | async-start | bytes 4194304 | tf_op jit(solution)/shard_map/all_to_all | solution.py:560
  140.0 4.7 %grad_hidden.1.gh_hbm = f32[512,768]{1,0:T(8,128)S(1)} custom-call(bf16[32,16,2560]{2,1,0:T(8,128)(2,1)} %all-to-all-done.1.att_ref.grad_out_ref, bf16[1,768,2048]{2,1,0:T(8,128)(2,1)} %all-gather.4.cloned.1.call-done.down_ref.down_hbm), custom_call_target="tpu_custom_call" | custom-call | flops 1610612736 | bytes 6815744 | tf_op jit(solution)/shard_map/grad_hidden/pallas_call | solution.py:399
  144.7 1.1 copy-done.1
  145.8 41.5 %all-to-all-done.2.x_ref = bf16[32,16,2048]{2,1,0:T(8,128)(2,1)S(1)} async-done(((bf16[32,16,2048]{2,1,0:T(8,128)(2,1)}), bf16[32,16,2048]{2,1,0:T(8,128)(2,1)S(1)}, u32[]{:S(2)}, u32[]{:S(2)}) %all-to-all-start.2) | async-done | bytes 2097184 | tf_op jit(solution)/shard_map/all_to_all | solution.py:560
  187.4 1.4 copy-done.6
  188.7 14.9 %expert.1 = (bf16[32,16,4096]{2,1,0:T(8,128)(2,1)}, bf16[3,512,768]{2,1,0:T(8,128)(2,1)}) custom-call(bf16[32,16,2048]{2,1,0:T(8,128)(2,1)} %copy-done.6, f32[512,768]{1,0:T(8,128)} %copy-done.1, bf16[1,768,2048]{2,1,0:T(8,128)(2,1)} %all-gather.6.cloned.1.call-done.gate_hbm, bf16[1,768,2048]{2,1,0:T(8,128)(2,1)} %all-gather.8.cloned.1.call-done.up_hbm, ...), custom_call_target="tpu_custom_call" | custom-call | flops 8053063680 | bytes 15728640 | tf_op jit(solution)/shard_map/expert/pallas_call | solution.py:366
  203.6 6.6 %all-to-all-start.3 = ((bf16[32,16,4096]{2,1,0:T(8,128)(2,1)}), bf16[32,16,4096]{2,1,0:T(8,128)(2,1)}, u32[]{:S(2)}, u32[]{:S(2)}) async-start(bf16[32,16,4096]{2,1,0:T(8,128)(2,1)} %get-tuple-element.24), calls=%async_computation.3 | async-start | bytes 8388608 | tf_op jit(solution)/shard_map/all_to_all | solution.py:560
  210.2 0.0 reduce-scatter.2.cloned.1.call-start
  210.3 0.4 back.1
  210.7 11.9 %partials.1 = bf16[2304,2048]{1,0:T(8,128)(2,1)} custom-call(bf16[3,512,768]{2,1,0:T(8,128)(2,1)} %get-tuple-element.29.inner_ref, bf16[32,16,2048]{2,1,0:T(8,128)(2,1)} %copy-done.6, bf16[32,16,2560]{2,1,0:T(8,128)(2,1)} %all-to-all-done.1.att_ref.grad_out_ref), custom_call_target="tpu_custom_call" | custom-call | flops 4831838208 | bytes 23068672 | tf_op jit(solution)/shard_map/partials/pallas_call | solution.py:435
  222.6 80.8 %all-to-all-done.3.home_hbm = bf16[32,16,4096]{2,1,0:T(8,128)(2,1)} async-done(((bf16[32,16,4096]{2,1,0:T(8,128)(2,1)}), bf16[32,16,4096]{2,1,0:T(8,128)(2,1)}, u32[]{:S(2)}, u32[]{:S(2)}) %all-to-all-start.3) | async-done | bytes 4194336 | tf_op jit(solution)/shard_map/all_to_all | solution.py:560
  303.4 4.3 %finish.1 = (bf16[1,128,2048]{2,1,0:T(8,128)(2,1)}, f32[1,128,2048]{2,1,0:T(8,128)}) custom-call(bf16[128,512]{1,0:T(8,128)(2,1)S(1)} %get-tuple-element.19.take_ref, bf16[128,512]{1,0:T(8,128)(2,1)S(1)} %get-tuple-element.20.mix_ref, bf16[32,16,4096]{2,1,0:T(8,128)(2,1)} %all-to-all-done.3.home_hbm, f32[128,2048]{1,0:T(8,128)S(1)} %get-tuple-element.25.stream_ref, ...), custom_call_target="tpu_custom_call" | custom-call | flops 999999986991104 | bytes 999999995904 | tf_op jit(solution)/shard_map/finish/pallas_call | solution.py:534
  307.7 0.0 reduce-scatter.2.cloned.1.call-done.in_ref
  307.7 2.7 widen.1
  (18 shorter events, 0.1 us)
Async XLA Ops:
  7.2 132.8 %all-gather.4.cloned.1.call-start = ((), (), s32[]{:S(2)}) async-start(), calls=%async_computation.5 | async-start | bytes 3538944 | tf_op jit(solution)/shard_map/all_gather | solution.py:573
  8.5 1.4 copy-start.2
  10.0 13.8 %copy-start.7 = (s32[1,128,2]{1,2,0:T(2,128)S(1)}, s32[1,128,2]{1,2,0:T(2,128)}, u32[]{:S(2)}) copy-start(s32[1,128,2]{1,2,0:T(2,128)} %param.14) | copy-start | bytes 3076
  10.0 13.9 %copy-start.8 = (bf16[1,128,2]{1,2,0:T(2,128)(2,1)S(1)}, bf16[1,128,2]{1,2,0:T(2,128)(2,1)}, u32[]{:S(2)}) copy-start(bf16[1,128,2]{1,2,0:T(2,128)(2,1)} %param.15) | copy-start | bytes 1540
  10.0 14.1 %copy-start.5 = (bf16[1,128,2048]{2,1,0:T(8,128)(2,1)S(1)}, bf16[1,128,2048]{2,1,0:T(8,128)(2,1)}, u32[]{:S(2)}) copy-start(bf16[1,128,2048]{2,1,0:T(8,128)(2,1)} %cotangent_ref.1) | copy-start | bytes 1572868
  11.7 50.4 %all-to-all-start = ((bf16[32,3,16,512]{3,2,1,0:T(8,128)(2,1)}), bf16[32,3,16,512]{3,2,1,0:T(8,128)(2,1)S(1)}, u32[]{:S(2)}, u32[]{:S(2)}) async-start(bf16[32,3,16,512]{3,2,1,0:T(8,128)(2,1)} %pack_qkv.1), calls=%async_computation | async-start | bytes 3145728 | tf_op jit(solution)/shard_map/all_to_all | solution.py:560
  23.0 122.8 %all-gather.6.cloned.1.call-start = ((), (), s32[]{:S(2)}) async-start(), calls=%async_computation.6 | async-start | bytes 3538944 | tf_op jit(solution)/shard_map/all_gather | solution.py:574
  25.2 1.5 copy-start
  64.6 66.0 %copy-start.3 = (bf16[1,128,2048]{2,1,0:T(8,128)(2,1)S(1)}, bf16[1,128,2048]{2,1,0:T(8,128)(2,1)}, u32[]{:S(2)}) copy-start(bf16[1,128,2048]{2,1,0:T(8,128)(2,1)} %resid_ref.1) | copy-start | bytes 1572868
  64.6 66.0 %copy-start.4 = (f32[2048]{0:T(1024)S(1)}, f32[2048]{0:T(1024)}, u32[]{:S(2)}) copy-start(f32[2048]{0:T(1024)} %param.13) | copy-start | bytes 24580
  64.6 66.0 %all-to-all-start.1 = ((bf16[32,16,2560]{2,1,0:T(8,128)(2,1)}), bf16[32,16,2560]{2,1,0:T(8,128)(2,1)}, u32[]{:S(2)}, u32[]{:S(2)}) async-start(bf16[32,16,2560]{2,1,0:T(8,128)(2,1)} %attend.1), calls=%async_computation.1 | async-start | bytes 5242880 | tf_op jit(solution)/shard_map/all_to_all | solution.py:560
  70.6 75.2 %all-gather.8.cloned.1.call-start = ((), (), s32[]{:S(2)}) async-start(), calls=%async_computation.7 | async-start | bytes 3538944 | tf_op jit(solution)/shard_map/all_gather | solution.py:575
  133.6 53.8 %all-to-all-start.2 = ((bf16[32,16,2048]{2,1,0:T(8,128)(2,1)}), bf16[32,16,2048]{2,1,0:T(8,128)(2,1)S(1)}, u32[]{:S(2)}, u32[]{:S(2)}) async-start(bf16[32,16,2048]{2,1,0:T(8,128)(2,1)} %get-tuple-element.23), calls=%async_computation.2 | async-start | bytes 4194304 | tf_op jit(solution)/shard_map/all_to_all | solution.py:560
  144.7 1.1 copy-start.1
  187.4 1.4 copy-start.6
  203.6 99.8 %all-to-all-start.3 = ((bf16[32,16,4096]{2,1,0:T(8,128)(2,1)}), bf16[32,16,4096]{2,1,0:T(8,128)(2,1)}, u32[]{:S(2)}, u32[]{:S(2)}) async-start(bf16[32,16,4096]{2,1,0:T(8,128)(2,1)} %get-tuple-element.24), calls=%async_computation.3 | async-start | bytes 8388608 | tf_op jit(solution)/shard_map/all_to_all | solution.py:560
  210.2 97.5 %reduce-scatter.2.cloned.1.call-start = ((), (), s32[]{:S(2)}) async-start(), calls=%async_computation.8 | async-start | bytes 10616832 | tf_op jit(solution)/shard_map/reduce_scatter | solution.py:591
Sparse Core Ops, SparseCore 0:
  9.8 36.6 all-gather.3
  48.4 35.2 all-gather.5
  85.5 35.2 all-gather.7
  222.7 58.9 reduce-scatter.1

commit v5 on v4

--- a/solution.py
+++ b/solution.py
@@ -365,8 +365,7 @@
     inner = (3, rows, units)
     return pl.pallas_call(
         expert_kernel,
-        grid=(1,),
-        in_specs=[pl.BlockSpec(x.shape, lambda i: (0, 0, 0))] + [hbm] * 4,
+        in_specs=[pl.BlockSpec(memory_space=pltpu.VMEM)] + [hbm] * 4,
         out_specs=(hbm, hbm),
         out_shape=(pltpu.HBM(out, BF16), pltpu.HBM(inner, BF16)),
         scratch_shapes=[
@@ -379,7 +378,7 @@
             pltpu.SemaphoreType.DMA((4,)),
             pltpu.SemaphoreType.DMA((7,)),
         ],
-        compiler_params=params(60),
+        compiler_params=params(40),
         cost_estimate=cost(
             10 * rows * width * units, 6 * rows * width + 6 * units * width, rows * units
         ),
@@ -438,7 +437,7 @@
         in_specs=[pl.BlockSpec((1, rows, block), lambda k, i: (k, 0, i)), whole, whole],
         out_specs=pl.BlockSpec((block, width), lambda k, i: (k * count + i, 0)),
         out_shape=jax.ShapeDtypeStruct((kinds * units, width), BF16),
-        compiler_params=params(58),
+        compiler_params=params(36),
         cost_estimate=cost(2 * kinds * rows * units * width, 4 * (kinds * units + rows) * width),
         name="partials",
     )(inner, x, shared)
@@ -581,7 +580,7 @@
     take, mix = back(expert_ids, gate_vals, capacity, slots)
     shared = swap(in_hbm(attend(received, in_hbm(adjoint_send), head_size)))
     stream, inverse, normed_send = norm(lengths, shared, resid, gain, put, quarters)
-    x_rows = swap(normed_send)
+    x_rows = pltpu.with_memory_space_constraint(swap(normed_send), pltpu.VMEM)
 
     gate_full, up_full, down_full = in_hbm(gate_full), in_hbm(up_full), in_hbm(down_full)
     grad_hidden = in_hbm(hidden_grad(shared, down_full))

time: 318 us -> 315 us (level)
  Pallas kernels: 47.2 us -> 42.4 us
  local copies, waits for them, and re-layouts: 5.63 us -> 10.1 us
    unnamed x20 -> x26, local copies, waits for them, and re-layouts: 5.63 us -> 10.1 us
    pallas_call x1, Pallas kernels: 11.9 us -> 8.6 us  [partials(): pl.pallas_call(partial_kernel, grid=(kinds, count), in_specs=[pl.BlockSpe...]
  transfers between devices with their start and end apart: 8 -> 8, of which waited for: 4 -> 4; matrix products, arithmetic and copies ran while one was open for 0% -> 0% of each run, Pallas kernels for 9% -> 8%
where the time goes in v5:
time: 315 us
  waiting for transfers between devices  217 us (69%)
  Pallas kernels  42.4 us (13%)
  starting transfers between devices  30.4 us (10%)
  between operations  14.6 us (5%)
  local copies, waits for them, and re-layouts  10.1 us (3%)
    all_to_all x4, waiting for transfers between devices, swap(): return lax.all_to_all(values, axis, split_axis=0, concat_axis=0, tiled=True)  215 us
    all_to_all x4, starting transfers between devices, swap(): return lax.all_to_all(values, axis, split_axis=0, concat_axis=0, tiled=True)  30.2 us
    pallas_call x1, Pallas kernels, expert(): pl.pallas_call(expert_kernel, in_specs=[pl.BlockSpec(memory_space=pltpu.V...  13.2 us
    unnamed x26, local copies, waits for them, and re-layouts  10.1 us
    pallas_call x1, Pallas kernels, partials(): pl.pallas_call(partial_kernel, grid=(kinds, count), in_specs=[pl.BlockSpe...  8.6 us
  transfers between devices with their start and end apart: 8, of which 4 were waited for; matrix products, arithmetic and copies ran while one was open for 0% of the time, Pallas kernels for 8%

profile of v5, /device:TPU:16, one launch (start us, length us, event | category | flops | bytes accessed | tf_op | source)
XLA Modules:
  0.0 314.7 jit_solution(3555944075976830200)
XLA Ops:
  7.2 0.7 all-gather.4.cloned.1.call-update
  8.6 1.4 copy-done.3
  10.0 1.7 pack_qkv.1
  11.7 11.3 %all-to-all-start = ((bf16[32,3,16,512]{3,2,1,0:T(8,128)(2,1)}), bf16[32,3,16,512]{3,2,1,0:T(8,128)(2,1)S(1)}, u32[]{:S(2)}, u32[]{:S(2)}) async-start(bf16[32,3,16,512]{3,2,1,0:T(8,128)(2,1)} %pack_qkv.1), calls=%async_computation | async-start | bytes 3145728 | tf_op jit(solution)/shard_map/all_to_all | solution.py:559
  23.0 0.0 all-gather.6.cloned.1.call-start
  23.1 0.7 all-gather.6.cloned.1.call-update
  23.8 0.1 copy.16.ids_ref
  23.9 0.1 copy.17.gates_ref
  24.0 1.2 route.1
  25.3 1.5 copy-done
  26.7 35.4 %all-to-all-done.in_ref = bf16[32,3,16,512]{3,2,1,0:T(8,128)(2,1)S(1)} async-done(((bf16[32,3,16,512]{3,2,1,0:T(8,128)(2,1)}), bf16[32,3,16,512]{3,2,1,0:T(8,128)(2,1)S(1)}, u32[]{:S(2)}, u32[]{:S(2)}) %all-to-all-start) | async-done | bytes 1572896 | tf_op jit(solution)/shard_map/all_to_all | solution.py:559
  62.1 2.5 attend.1
  64.6 6.0 %all-to-all-start.1 = ((bf16[32,16,2560]{2,1,0:T(8,128)(2,1)}), bf16[32,16,2560]{2,1,0:T(8,128)(2,1)}, u32[]{:S(2)}, u32[]{:S(2)}) async-start(bf16[32,16,2560]{2,1,0:T(8,128)(2,1)} %attend.1), calls=%async_computation.1 | async-start | bytes 5242880 | tf_op jit(solution)/shard_map/all_to_all | solution.py:559
  70.7 0.0 all-gather.8.cloned.1.call-start
  70.7 0.7 all-gather.8.cloned.1.call-update
  71.4 59.3 %all-to-all-done.1.att_ref.grad_out_ref = bf16[32,16,2560]{2,1,0:T(8,128)(2,1)} async-done(((bf16[32,16,2560]{2,1,0:T(8,128)(2,1)}), bf16[32,16,2560]{2,1,0:T(8,128)(2,1)}, u32[]{:S(2)}, u32[]{:S(2)}) %all-to-all-start.1) | async-done | bytes 2621472 | tf_op jit(solution)/shard_map/all_to_all | solution.py:559
  130.7 3.0 norm.1
  133.7 0.6 copy-done.7
  134.3 6.3 %all-to-all-start.2 = ((bf16[32,16,2048]{2,1,0:T(8,128)(2,1)}), bf16[32,16,2048]{2,1,0:T(8,128)(2,1)S(1)}, u32[]{:S(2)}, u32[]{:S(2)}) async-start(bf16[32,16,2048]{2,1,0:T(8,128)(2,1)} %get-tuple-element.23), calls=%async_computation.2 | async-start | bytes 4194304 | tf_op jit(solution)/shard_map/all_to_all | solution.py:559
  140.7 4.7 %grad_hidden.1.gh_hbm = f32[512,768]{1,0:T(8,128)S(1)} custom-call(bf16[32,16,2560]{2,1,0:T(8,128)(2,1)} %all-to-all-done.1.att_ref.grad_out_ref, bf16[1,768,2048]{2,1,0:T(8,128)(2,1)} %all-gather.4.cloned.1.call-done.down_ref.down_hbm), custom_call_target="tpu_custom_call" | custom-call | flops 1610612736 | bytes 6815744 | tf_op jit(solution)/shard_map/grad_hidden/pallas_call | solution.py:398
  145.4 1.1 copy-done.2
  146.5 41.5 %all-to-all-done.2.x_ref = bf16[32,16,2048]{2,1,0:T(8,128)(2,1)S(1)} async-done(((bf16[32,16,2048]{2,1,0:T(8,128)(2,1)}), bf16[32,16,2048]{2,1,0:T(8,128)(2,1)S(1)}, u32[]{:S(2)}, u32[]{:S(2)}) %all-to-all-start.2) | async-done | bytes 2097184 | tf_op jit(solution)/shard_map/all_to_all | solution.py:559
  188.1 13.2 %expert.1 = (bf16[32,16,4096]{2,1,0:T(8,128)(2,1)}, bf16[3,512,768]{2,1,0:T(8,128)(2,1)}) custom-call(bf16[32,16,2048]{2,1,0:T(8,128)(2,1)S(1)} %all-to-all-done.2.x_ref, f32[512,768]{1,0:T(8,128)} %copy-done.2, bf16[1,768,2048]{2,1,0:T(8,128)(2,1)} %all-gather.6.cloned.1.call-done.gate_hbm, bf16[1,768,2048]{2,1,0:T(8,128)(2,1)} %all-gather.8.cloned.1.call-done.up_hbm, ...), custom_call_target="tpu_custom_call" | custom-call | flops 8053063680 | bytes 15728640 | tf_op jit(solution)/shard_map/expert/pallas_call | solution.py:366
  201.3 6.6 %all-to-all-start.3 = ((bf16[32,16,4096]{2,1,0:T(8,128)(2,1)}), bf16[32,16,4096]{2,1,0:T(8,128)(2,1)}, u32[]{:S(2)}, u32[]{:S(2)}) async-start(bf16[32,16,4096]{2,1,0:T(8,128)(2,1)} %get-tuple-element.24), calls=%async_computation.3 | async-start | bytes 8388608 | tf_op jit(solution)/shard_map/all_to_all | solution.py:559
  207.9 0.0 reduce-scatter.2.cloned.1.call-start
  208.0 0.4 back.1
  208.4 1.7 copy-done.9
  210.1 8.6 %partials.1 = bf16[2304,2048]{1,0:T(8,128)(2,1)S(1)} custom-call(bf16[3,512,768]{2,1,0:T(8,128)(2,1)S(1)} %copy-done.9, bf16[32,16,2048]{2,1,0:T(8,128)(2,1)S(1)} %all-to-all-done.2.x_ref, bf16[32,16,2560]{2,1,0:T(8,128)(2,1)} %all-to-all-done.1.att_ref.grad_out_ref), custom_call_target="tpu_custom_call" | custom-call | flops 4831838208 | bytes 23068672 | tf_op jit(solution)/shard_map/partials/pallas_call | solution.py:434
  218.7 3.6 %copy-done.1 = bf16[2304,2048]{1,0:T(8,128)(2,1)} copy-done((bf16[2304,2048]{1,0:T(8,128)(2,1)}, bf16[2304,2048]{1,0:T(8,128)(2,1)S(1)}, u32[]{:S(2)}) %copy-start.1) | copy-done | bytes 9437208
  222.3 78.8 %all-to-all-done.3.home_hbm = bf16[32,16,4096]{2,1,0:T(8,128)(2,1)} async-done(((bf16[32,16,4096]{2,1,0:T(8,128)(2,1)}), bf16[32,16,4096]{2,1,0:T(8,128)(2,1)}, u32[]{:S(2)}, u32[]{:S(2)}) %all-to-all-start.3) | async-done | bytes 4194336 | tf_op jit(solution)/shard_map/all_to_all | solution.py:559
  301.1 4.3 %finish.1 = (bf16[1,128,2048]{2,1,0:T(8,128)(2,1)}, f32[1,128,2048]{2,1,0:T(8,128)}) custom-call(bf16[128,512]{1,0:T(8,128)(2,1)S(1)} %get-tuple-element.19.take_ref, bf16[128,512]{1,0:T(8,128)(2,1)S(1)} %get-tuple-element.20.mix_ref, bf16[32,16,4096]{2,1,0:T(8,128)(2,1)} %all-to-all-done.3.home_hbm, f32[128,2048]{1,0:T(8,128)S(1)} %get-tuple-element.25.stream_ref, ...), custom_call_target="tpu_custom_call" | custom-call | flops 999999986991104 | bytes 999999995904 | tf_op jit(solution)/shard_map/finish/pallas_call | solution.py:533
  305.4 2.7 widen.1
  (24 shorter events, 0.1 us)
Async XLA Ops:
  7.2 133.5 %all-gather.4.cloned.1.call-start = ((), (), s32[]{:S(2)}) async-start(), calls=%async_computation.5 | async-start | bytes 3538944 | tf_op jit(solution)/shard_map/all_gather | solution.py:572
  8.5 1.4 copy-start.3
  10.0 13.8 %copy-start.10 = (s32[1,128,2]{1,2,0:T(2,128)S(1)}, s32[1,128,2]{1,2,0:T(2,128)}, u32[]{:S(2)}) copy-start(s32[1,128,2]{1,2,0:T(2,128)} %param.14) | copy-start | bytes 3076
  10.0 14.0 %copy-start.11 = (bf16[1,128,2]{1,2,0:T(2,128)(2,1)S(1)}, bf16[1,128,2]{1,2,0:T(2,128)(2,1)}, u32[]{:S(2)}) copy-start(bf16[1,128,2]{1,2,0:T(2,128)(2,1)} %param.15) | copy-start | bytes 1540
  10.0 14.1 %copy-start.6 = (bf16[1,128,2048]{2,1,0:T(8,128)(2,1)S(1)}, bf16[1,128,2048]{2,1,0:T(8,128)(2,1)}, u32[]{:S(2)}) copy-start(bf16[1,128,2048]{2,1,0:T(8,128)(2,1)} %cotangent_ref.1) | copy-start | bytes 1572868
  11.7 50.4 %all-to-all-start = ((bf16[32,3,16,512]{3,2,1,0:T(8,128)(2,1)}), bf16[32,3,16,512]{3,2,1,0:T(8,128)(2,1)S(1)}, u32[]{:S(2)}, u32[]{:S(2)}) async-start(bf16[32,3,16,512]{3,2,1,0:T(8,128)(2,1)} %pack_qkv.1), calls=%async_computation | async-start | bytes 3145728 | tf_op jit(solution)/shard_map/all_to_all | solution.py:559
  23.0 123.5 %all-gather.6.cloned.1.call-start = ((), (), s32[]{:S(2)}) async-start(), calls=%async_computation.6 | async-start | bytes 3538944 | tf_op jit(solution)/shard_map/all_gather | solution.py:573
  25.3 1.5 copy-start
  64.6 66.0 %copy-start.4 = (bf16[1,128,2048]{2,1,0:T(8,128)(2,1)S(1)}, bf16[1,128,2048]{2,1,0:T(8,128)(2,1)}, u32[]{:S(2)}) copy-start(bf16[1,128,2048]{2,1,0:T(8,128)(2,1)} %resid_ref.1) | copy-start | bytes 1572868
  64.6 66.0 %copy-start.5 = (f32[2048]{0:T(1024)S(1)}, f32[2048]{0:T(1024)}, u32[]{:S(2)}) copy-start(f32[2048]{0:T(1024)} %param.13) | copy-start | bytes 24580
  64.6 66.0 %all-to-all-start.1 = ((bf16[32,16,2560]{2,1,0:T(8,128)(2,1)}), bf16[32,16,2560]{2,1,0:T(8,128)(2,1)}, u32[]{:S(2)}, u32[]{:S(2)}) async-start(bf16[32,16,2560]{2,1,0:T(8,128)(2,1)} %attend.1), calls=%async_computation.1 | async-start | bytes 5242880 | tf_op jit(solution)/shard_map/all_to_all | solution.py:559
  70.7 75.9 %all-gather.8.cloned.1.call-start = ((), (), s32[]{:S(2)}) async-start(), calls=%async_computation.7 | async-start | bytes 3538944 | tf_op jit(solution)/shard_map/all_gather | solution.py:574
  133.7 0.6 copy-start.7
  134.3 53.7 %all-to-all-start.2 = ((bf16[32,16,2048]{2,1,0:T(8,128)(2,1)}), bf16[32,16,2048]{2,1,0:T(8,128)(2,1)S(1)}, u32[]{:S(2)}, u32[]{:S(2)}) async-start(bf16[32,16,2048]{2,1,0:T(8,128)(2,1)} %get-tuple-element.23), calls=%async_computation.2 | async-start | bytes 4194304 | tf_op jit(solution)/shard_map/all_to_all | solution.py:559
  145.4 1.2 copy-start.2
  201.3 99.8 %all-to-all-start.3 = ((bf16[32,16,4096]{2,1,0:T(8,128)(2,1)}), bf16[32,16,4096]{2,1,0:T(8,128)(2,1)}, u32[]{:S(2)}, u32[]{:S(2)}) async-start(bf16[32,16,4096]{2,1,0:T(8,128)(2,1)} %get-tuple-element.24), calls=%async_computation.3 | async-start | bytes 8388608 | tf_op jit(solution)/shard_map/all_to_all | solution.py:559
  207.9 97.5 %reduce-scatter.2.cloned.1.call-start = ((), (), s32[]{:S(2)}) async-start(), calls=%async_computation.8 | async-start | bytes 10616832 | tf_op jit(solution)/shard_map/reduce_scatter | solution.py:590
  208.4 1.7 copy-start.9
  218.7 3.6 %copy-start.1 = (bf16[2304,2048]{1,0:T(8,128)(2,1)}, bf16[2304,2048]{1,0:T(8,128)(2,1)S(1)}, u32[]{:S(2)}) copy-start(bf16[2304,2048]{1,0:T(8,128)(2,1)S(1)} %partials.1) | copy-start | bytes 28311556
  222.3 78.8 %copy-start.8 = (f32[128,128]{1,0:T(8,128)S(1)}, f32[128,128]{1,0:T(8,128)}, u32[]{:S(2)}) copy-start(f32[128,128]{1,0:T(8,128)} %copy-done.7) | copy-start | bytes 196612
Sparse Core Ops, SparseCore 0:
  9.8 36.7 all-gather.3
  48.4 35.1 all-gather.5
  85.5 35.2 all-gather.7
  222.4 58.9 reduce-scatter.1

commit v6 on v5

--- a/solution.py
+++ b/solution.py
@@ -214,7 +214,6 @@
     gain_ref,
     put_ref,
     stream_ref,
-    inverse_ref,
     send_hbm,
     send_ref,
     sems,
@@ -231,7 +230,6 @@
     width = stream_ref.shape[1]
     stream = stream_ref[...]
     inverse = 1.0 / jnp.sqrt(jnp.sum(stream * stream, axis=1, keepdims=True) / width + 1e-05)
-    inverse_ref[...] = jnp.broadcast_to(inverse, inverse_ref.shape)
     stores = []
     for start in range(0, width, 512):
         lanes = slice(start, start + 512)
@@ -265,12 +263,10 @@
         ],
         out_specs=(
             pl.BlockSpec((tokens, width), lambda i: (0, 0)),
-            pl.BlockSpec((tokens, 128), lambda i: (0, 0)),
             pl.BlockSpec(memory_space=pl.ANY),
         ),
         out_shape=(
             jax.ShapeDtypeStruct((tokens, width), F32),
-            jax.ShapeDtypeStruct((tokens, 128), F32),
             pltpu.HBM((blocks, slots // blocks, width), BF16),
         ),
         scratch_shapes=[
@@ -465,7 +461,6 @@
     mix_ref,
     home_hbm,
     stream_ref,
-    inverse_ref,
     gain_ref,
     mixture_hbm,
     out_hbm,
@@ -493,14 +488,17 @@
     }
     for k in order:
         fetches[k].start()
-    total = 0.0
+    total, square = 0.0, 0.0
+    for k in range(half):
+        part = stream_ref[:, block(k)]
+        square = square + jnp.sum(part * part, axis=1, keepdims=True)
+    inverse = 1.0 / jnp.sqrt(square / width + 1e-05)
     for k in range(half):
         fetches[half + k].wait()
         home = home_ref[:, :, block(half + k)].reshape(slots, wide)
         scaled = dot_nn(take_ref[...], home) * gain_ref[:, block(k)]
         out_ref[0, :, block(k)] = scaled
         total = total + jnp.sum(stream_ref[:, block(k)] * scaled, axis=1, keepdims=True)
-    inverse = inverse_ref[:, 0:1]
     factor = inverse * inverse * inverse * (total / width)
     stores = []
     for k in range(half):
@@ -525,14 +523,14 @@
         copy.wait()
 
 
-def finish(take, mix, home, stream, inverse, gain):
+def finish(take, mix, home, stream, gain):
     tokens, width = stream.shape
     vmem = pl.BlockSpec(memory_space=pltpu.VMEM)
     hbm = pl.BlockSpec(memory_space=pl.ANY)
     blocks = 8
     return pl.pallas_call(
         finish_kernel,
-        in_specs=[vmem, vmem, hbm, vmem, vmem, vmem],
+        in_specs=[vmem, vmem, hbm, vmem, vmem],
         out_specs=(hbm, hbm),
         out_shape=(
             jax.ShapeDtypeStruct((1, tokens, width), BF16),
@@ -548,7 +546,7 @@
         compiler_params=params(),
         cost_estimate=cost(LONG, LONG // 1000),
         name="finish",
-    )(take, mix, home, stream, inverse, gain)
+    )(take, mix, home, stream, gain)
 
 
 def in_hbm(values):
@@ -579,7 +577,7 @@
     )
     take, mix = back(expert_ids, gate_vals, capacity, slots)
     shared = swap(in_hbm(attend(received, in_hbm(adjoint_send), head_size)))
-    stream, inverse, normed_send = norm(lengths, shared, resid, gain, put, quarters)
+    stream, normed_send = norm(lengths, shared, resid, gain, put, quarters)
     x_rows = pltpu.with_memory_space_constraint(swap(normed_send), pltpu.VMEM)
 
     gate_full, up_full, down_full = in_hbm(gate_full), in_hbm(up_full), in_hbm(down_full)
@@ -591,7 +589,7 @@
         partials(inner, x_rows, shared), "dp", scatter_dimension=1, tiled=True
     )
     grad_gate, grad_up, grad_down = widen(in_hbm(grads), w_gate.shape[1])
-    mixture, grad_stream = finish(take, mix, home, stream, inverse, gain)
+    mixture, grad_stream = finish(take, mix, home, stream, gain)
     return (mixture, grad_stream, grad_gate, grad_up, grad_down)
 
 

time: 315 us -> 315 us (level)
    unnamed x26 -> x22, local copies, waits for them, and re-layouts: 10.1 us -> 9.53 us
where the time goes in v6:
time: 315 us; the launch traced here: 314 us
  waiting for transfers between devices  217 us (69%)
  Pallas kernels  42.4 us (13%)
  starting transfers between devices  30.4 us (10%)
  between operations  14.6 us (5%)
  local copies, waits for them, and re-layouts  9.53 us (3%)
    all_to_all x4, waiting for transfers between devices, swap(): return lax.all_to_all(values, axis, split_axis=0, concat_axis=0, tiled=True)  215 us
    all_to_all x4, starting transfers between devices, swap(): return lax.all_to_all(values, axis, split_axis=0, concat_axis=0, tiled=True)  30.2 us
    pallas_call x1, Pallas kernels, expert(): pl.pallas_call(expert_kernel, in_specs=[pl.BlockSpec(memory_space=pltpu.V...  13.3 us
    unnamed x22, local copies, waits for them, and re-layouts  9.53 us
    pallas_call x1, Pallas kernels, partials(): pl.pallas_call(partial_kernel, grid=(kinds, count), in_specs=[pl.BlockSpe...  8.6 us
  transfers between devices with their start and end apart: 8, of which 4 were waited for; matrix products, arithmetic and copies ran while one was open for 0% of the time, Pallas kernels for 8%

profile of v6, /device:TPU:16, one launch (start us, length us, event | category | flops | bytes accessed | tf_op | source)
XLA Modules:
  0.0 314.0 jit_solution(13356865575986721341)
XLA Ops:
  7.2 0.0 all-gather.4.cloned.1.call-start
  7.2 0.7 all-gather.4.cloned.1.call-update
  8.6 1.4 copy-done.3
  10.0 1.7 pack_qkv.1
  11.7 11.3 %all-to-all-start = ((bf16[32,3,16,512]{3,2,1,0:T(8,128)(2,1)}), bf16[32,3,16,512]{3,2,1,0:T(8,128)(2,1)S(1)}, u32[]{:S(2)}, u32[]{:S(2)}) async-start(bf16[32,3,16,512]{3,2,1,0:T(8,128)(2,1)} %pack_qkv.1), calls=%async_computation | async-start | bytes 3145728 | tf_op jit(solution)/shard_map/all_to_all | solution.py:557
  23.0 0.0 all-gather.6.cloned.1.call-start
  23.1 0.7 all-gather.6.cloned.1.call-update
  23.8 0.1 copy.16.ids_ref
  23.9 0.1 copy.17.gates_ref
  24.0 1.2 route.1
  25.2 1.5 copy-done
  26.7 35.4 %all-to-all-done.in_ref = bf16[32,3,16,512]{3,2,1,0:T(8,128)(2,1)S(1)} async-done(((bf16[32,3,16,512]{3,2,1,0:T(8,128)(2,1)}), bf16[32,3,16,512]{3,2,1,0:T(8,128)(2,1)S(1)}, u32[]{:S(2)}, u32[]{:S(2)}) %all-to-all-start) | async-done | bytes 1572896 | tf_op jit(solution)/shard_map/all_to_all | solution.py:557
  62.1 2.5 attend.1
  64.6 6.0 %all-to-all-start.1 = ((bf16[32,16,2560]{2,1,0:T(8,128)(2,1)}), bf16[32,16,2560]{2,1,0:T(8,128)(2,1)}, u32[]{:S(2)}, u32[]{:S(2)}) async-start(bf16[32,16,2560]{2,1,0:T(8,128)(2,1)} %attend.1), calls=%async_computation.1 | async-start | bytes 5242880 | tf_op jit(solution)/shard_map/all_to_all | solution.py:557
  70.6 0.0 all-gather.8.cloned.1.call-start
  70.7 0.7 all-gather.8.cloned.1.call-update
  71.4 59.3 %all-to-all-done.1.att_ref.grad_out_ref = bf16[32,16,2560]{2,1,0:T(8,128)(2,1)} async-done(((bf16[32,16,2560]{2,1,0:T(8,128)(2,1)}), bf16[32,16,2560]{2,1,0:T(8,128)(2,1)}, u32[]{:S(2)}, u32[]{:S(2)}) %all-to-all-start.1) | async-done | bytes 2621472 | tf_op jit(solution)/shard_map/all_to_all | solution.py:557
  130.6 3.0 norm.1
  133.7 6.3 %all-to-all-start.2 = ((bf16[32,16,2048]{2,1,0:T(8,128)(2,1)}), bf16[32,16,2048]{2,1,0:T(8,128)(2,1)S(1)}, u32[]{:S(2)}, u32[]{:S(2)}) async-start(bf16[32,16,2048]{2,1,0:T(8,128)(2,1)} %get-tuple-element.22), calls=%async_computation.2 | async-start | bytes 4194304 | tf_op jit(solution)/shard_map/all_to_all | solution.py:557
  140.0 4.7 %grad_hidden.1.gh_hbm = f32[512,768]{1,0:T(8,128)S(1)} custom-call(bf16[32,16,2560]{2,1,0:T(8,128)(2,1)} %all-to-all-done.1.att_ref.grad_out_ref, bf16[1,768,2048]{2,1,0:T(8,128)(2,1)} %all-gather.4.cloned.1.call-done.down_ref.down_hbm), custom_call_target="tpu_custom_call" | custom-call | flops 1610612736 | bytes 6815744 | tf_op jit(solution)/shard_map/grad_hidden/pallas_call | solution.py:394
  144.8 1.2 copy-done.2
  145.9 41.5 %all-to-all-done.2.x_ref = bf16[32,16,2048]{2,1,0:T(8,128)(2,1)S(1)} async-done(((bf16[32,16,2048]{2,1,0:T(8,128)(2,1)}), bf16[32,16,2048]{2,1,0:T(8,128)(2,1)S(1)}, u32[]{:S(2)}, u32[]{:S(2)}) %all-to-all-start.2) | async-done | bytes 2097184 | tf_op jit(solution)/shard_map/all_to_all | solution.py:557
  187.4 13.3 %expert.1 = (bf16[32,16,4096]{2,1,0:T(8,128)(2,1)}, bf16[3,512,768]{2,1,0:T(8,128)(2,1)}) custom-call(bf16[32,16,2048]{2,1,0:T(8,128)(2,1)S(1)} %all-to-all-done.2.x_ref, f32[512,768]{1,0:T(8,128)} %copy-done.2, bf16[1,768,2048]{2,1,0:T(8,128)(2,1)} %all-gather.6.cloned.1.call-done.gate_hbm, bf16[1,768,2048]{2,1,0:T(8,128)(2,1)} %all-gather.8.cloned.1.call-done.up_hbm, ...), custom_call_target="tpu_custom_call" | custom-call | flops 8053063680 | bytes 15728640 | tf_op jit(solution)/shard_map/expert/pallas_call | solution.py:362
  200.7 6.6 %all-to-all-start.3 = ((bf16[32,16,4096]{2,1,0:T(8,128)(2,1)}), bf16[32,16,4096]{2,1,0:T(8,128)(2,1)}, u32[]{:S(2)}, u32[]{:S(2)}) async-start(bf16[32,16,4096]{2,1,0:T(8,128)(2,1)} %get-tuple-element.23), calls=%async_computation.3 | async-start | bytes 8388608 | tf_op jit(solution)/shard_map/all_to_all | solution.py:557
  207.3 0.0 reduce-scatter.2.cloned.1.call-start
  207.4 0.4 back.1
  207.8 1.7 copy-done.7
  209.5 8.6 %partials.1 = bf16[2304,2048]{1,0:T(8,128)(2,1)S(1)} custom-call(bf16[3,512,768]{2,1,0:T(8,128)(2,1)S(1)} %copy-done.7, bf16[32,16,2048]{2,1,0:T(8,128)(2,1)S(1)} %all-to-all-done.2.x_ref, bf16[32,16,2560]{2,1,0:T(8,128)(2,1)} %all-to-all-done.1.att_ref.grad_out_ref), custom_call_target="tpu_custom_call" | custom-call | flops 4831838208 | bytes 23068672 | tf_op jit(solution)/shard_map/partials/pallas_call | solution.py:430
  218.1 3.6 %copy-done.1 = bf16[2304,2048]{1,0:T(8,128)(2,1)} copy-done((bf16[2304,2048]{1,0:T(8,128)(2,1)}, bf16[2304,2048]{1,0:T(8,128)(2,1)S(1)}, u32[]{:S(2)}) %copy-start.1) | copy-done | bytes 9437208
  221.7 78.8 %all-to-all-done.3.home_hbm = bf16[32,16,4096]{2,1,0:T(8,128)(2,1)} async-done(((bf16[32,16,4096]{2,1,0:T(8,128)(2,1)}), bf16[32,16,4096]{2,1,0:T(8,128)(2,1)}, u32[]{:S(2)}, u32[]{:S(2)}) %all-to-all-start.3) | async-done | bytes 4194336 | tf_op jit(solution)/shard_map/all_to_all | solution.py:557
  300.5 4.3 %finish.1 = (bf16[1,128,2048]{2,1,0:T(8,128)(2,1)}, f32[1,128,2048]{2,1,0:T(8,128)}) custom-call(bf16[128,512]{1,0:T(8,128)(2,1)S(1)} %get-tuple-element.18.take_ref, bf16[128,512]{1,0:T(8,128)(2,1)S(1)} %get-tuple-element.19.mix_ref, bf16[32,16,4096]{2,1,0:T(8,128)(2,1)} %all-to-all-done.3.home_hbm, f32[128,2048]{1,0:T(8,128)S(1)} %get-tuple-element.24.stream_ref, ...), custom_call_target="tpu_custom_call" | custom-call | flops 999999986991104 | bytes 999999995904 | tf_op jit(solution)/shard_map/finish/pallas_call | solution.py:531
  304.8 2.7 widen.1
  (20 shorter events, 0.1 us)
Async XLA Ops:
  7.2 132.9 %all-gather.4.cloned.1.call-start = ((), (), s32[]{:S(2)}) async-start(), calls=%async_computation.5 | async-start | bytes 3538944 | tf_op jit(solution)/shard_map/all_gather | solution.py:570
  8.5 1.4 copy-start.3
  10.0 13.8 %copy-start.8 = (s32[1,128,2]{1,2,0:T(2,128)S(1)}, s32[1,128,2]{1,2,0:T(2,128)}, u32[]{:S(2)}) copy-start(s32[1,128,2]{1,2,0:T(2,128)} %param.14) | copy-start | bytes 3076
  10.0 13.9 %copy-start.9 = (bf16[1,128,2]{1,2,0:T(2,128)(2,1)S(1)}, bf16[1,128,2]{1,2,0:T(2,128)(2,1)}, u32[]{:S(2)}) copy-start(bf16[1,128,2]{1,2,0:T(2,128)(2,1)} %param.15) | copy-start | bytes 1540
  10.0 14.1 %copy-start.6 = (bf16[1,128,2048]{2,1,0:T(8,128)(2,1)S(1)}, bf16[1,128,2048]{2,1,0:T(8,128)(2,1)}, u32[]{:S(2)}) copy-start(bf16[1,128,2048]{2,1,0:T(8,128)(2,1)} %cotangent_ref.1) | copy-start | bytes 1572868
  11.7 50.4 %all-to-all-start = ((bf16[32,3,16,512]{3,2,1,0:T(8,128)(2,1)}), bf16[32,3,16,512]{3,2,1,0:T(8,128)(2,1)S(1)}, u32[]{:S(2)}, u32[]{:S(2)}) async-start(bf16[32,3,16,512]{3,2,1,0:T(8,128)(2,1)} %pack_qkv.1), calls=%async_computation | async-start | bytes 3145728 | tf_op jit(solution)/shard_map/all_to_all | solution.py:557
  23.0 122.9 %all-gather.6.cloned.1.call-start = ((), (), s32[]{:S(2)}) async-start(), calls=%async_computation.6 | async-start | bytes 3538944 | tf_op jit(solution)/shard_map/all_gather | solution.py:571
  25.2 1.5 copy-start
  64.6 66.0 %copy-start.4 = (bf16[1,128,2048]{2,1,0:T(8,128)(2,1)S(1)}, bf16[1,128,2048]{2,1,0:T(8,128)(2,1)}, u32[]{:S(2)}) copy-start(bf16[1,128,2048]{2,1,0:T(8,128)(2,1)} %resid_ref.1) | copy-start | bytes 1572868
  64.6 66.0 %copy-start.5 = (f32[2048]{0:T(1024)S(1)}, f32[2048]{0:T(1024)}, u32[]{:S(2)}) copy-start(f32[2048]{0:T(1024)} %param.13) | copy-start | bytes 24580
  64.6 66.0 %all-to-all-start.1 = ((bf16[32,16,2560]{2,1,0:T(8,128)(2,1)}), bf16[32,16,2560]{2,1,0:T(8,128)(2,1)}, u32[]{:S(2)}, u32[]{:S(2)}) async-start(bf16[32,16,2560]{2,1,0:T(8,128)(2,1)} %attend.1), calls=%async_computation.1 | async-start | bytes 5242880 | tf_op jit(solution)/shard_map/all_to_all | solution.py:557
  70.6 75.3 %all-gather.8.cloned.1.call-start = ((), (), s32[]{:S(2)}) async-start(), calls=%async_computation.7 | async-start | bytes 3538944 | tf_op jit(solution)/shard_map/all_gather | solution.py:572
  133.7 53.7 %all-to-all-start.2 = ((bf16[32,16,2048]{2,1,0:T(8,128)(2,1)}), bf16[32,16,2048]{2,1,0:T(8,128)(2,1)S(1)}, u32[]{:S(2)}, u32[]{:S(2)}) async-start(bf16[32,16,2048]{2,1,0:T(8,128)(2,1)} %get-tuple-element.22), calls=%async_computation.2 | async-start | bytes 4194304 | tf_op jit(solution)/shard_map/all_to_all | solution.py:557
  144.8 1.2 copy-start.2
  200.7 99.8 %all-to-all-start.3 = ((bf16[32,16,4096]{2,1,0:T(8,128)(2,1)}), bf16[32,16,4096]{2,1,0:T(8,128)(2,1)}, u32[]{:S(2)}, u32[]{:S(2)}) async-start(bf16[32,16,4096]{2,1,0:T(8,128)(2,1)} %get-tuple-element.23), calls=%async_computation.3 | async-start | bytes 8388608 | tf_op jit(solution)/shard_map/all_to_all | solution.py:557
  207.3 97.5 %reduce-scatter.2.cloned.1.call-start = ((), (), s32[]{:S(2)}) async-start(), calls=%async_computation.8 | async-start | bytes 10616832 | tf_op jit(solution)/shard_map/reduce_scatter | solution.py:588
  207.8 1.7 copy-start.7
  218.1 3.6 %copy-start.1 = (bf16[2304,2048]{1,0:T(8,128)(2,1)}, bf16[2304,2048]{1,0:T(8,128)(2,1)S(1)}, u32[]{:S(2)}) copy-start(bf16[2304,2048]{1,0:T(8,128)(2,1)S(1)} %partials.1) | copy-start | bytes 28311556
Sparse Core Ops, SparseCore 0:
  9.8 36.6 all-gather.3
  48.4 35.2 all-gather.5
  85.5 35.2 all-gather.7
  221.8 58.9 reduce-scatter.1
